TPU v7x, 32 devices: a whole 2x2x4 slice. The times are simulated.
32 devices in a mesh: groups: 2 (over y), section: 2 (over core), row: 2 (over x), col: 4 (over z).
Axes of the slice: x: 2, y: 2, z: 4, core: 2. Of those that a mesh axis runs over, the one named last changes fastest.
Arguments:
- hidden: bfloat16 [2, 2, 3072, 8192], P('section', None, ('groups', 'col'), 'row'), parts along dimension 2, may hold values from -400 to 400
- upstream: bfloat16 [2, 3072, 8192], P(None, ('groups', 'col'), 'row'), parts along dimension 1, may hold values from -8 to 8
- weights: bfloat16 [2, 8192, 8192], P('section', 'row', 'col'), may hold values from -0.0625 to 0.0625
- norm_gains: bfloat16 [2, 8192], P('section', 'row'), may hold values from 0.5 to 1.5
- steering: bfloat16 [16384], P(('groups', 'row')), parts along dimension 0, may hold values from -18 to 18
- steer_layer: int32 [2, 3072], P(None, ('groups', 'col')), parts along dimension 1, may hold values from 0 to 1
Outputs:
- section_grads: bfloat16 [2, 2, 3072, 8192], P('section', None, ('groups', 'col'), 'row'), parts along dimension 2
- steer_grad: float32 [16384], P(('groups', 'row')), parts along dimension 0
There are 2 independent parts, one for each index of `groups`. A program takes and returns all parts, laid end to end along the dimension named above; an argument that names none is the same for every part. Nothing has to cross between parts.
All inputs are finite; a program needn't handle non-finite values.
Results may differ from a plain program's by a relative error of at most 0.0038.
Values may be sent and summed in bfloat16 or wider, within the bound.
A program may use at most 320 MiB of HBM per device.

v0:
```python
import jax
import jax.numpy as jnp
from jax import lax
from jax.sharding import PartitionSpec as P

D = 8192
ROWS = 1536
MICRO = 2


epsilon = 1e-06


def passed_along(value, axis, steps):
    count = lax.axis_size(axis)
    initial, last = (max(0, -steps), min(count, count - steps))
    return lax.ppermute(value, axis, [(source, source + steps) for source in range(initial, last)])


def local(hidden, upstream, weights, norm_gains, steering, steer_layer):
    sections = lax.axis_size("section")
    section_index = lax.axis_index("section")
    scaling = norm_gains[0].astype(jnp.float32)
    steer_vec = steering.astype(jnp.float32)
    unsteered_all = hidden[0].astype(jnp.float32)
    moved_all = unsteered_all + steer_vec
    row_count = unsteered_all.shape[1]
    feature_count = unsteered_all.shape[2]
    local_weight = weights[0]
    contract = (((1,), (1,)), ((), ()))
    full_weight = lax.all_gather(local_weight, "col", axis=1, tiled=True)
    ticks = MICRO + sections - 1
    received = jnp.zeros((row_count, feature_count), jnp.bfloat16)
    results = jnp.zeros((MICRO, row_count, feature_count), jnp.bfloat16)
    steer_part = jnp.zeros((feature_count,), jnp.float32)
    slots = jnp.arange(MICRO, dtype=jnp.int32)
    for tick_index in range(ticks):
        micro_index = tick_index - (sections - 1 - section_index)
        active = (micro_index >= 0) & (micro_index < MICRO)
        clipped = jnp.clip(micro_index, 0, MICRO - 1)
        if tick_index < MICRO:
            upstream_block = upstream[tick_index]
        else:
            upstream_block = jnp.zeros_like(upstream[0])
        grad_in = jnp.where(section_index == sections - 1, upstream_block, received)
        unsteered = lax.dynamic_index_in_dim(unsteered_all, clipped, 0, keepdims=False)
        moved = lax.dynamic_index_in_dim(moved_all, clipped, 0, keepdims=False)
        layer_rows = lax.dynamic_index_in_dim(steer_layer, clipped, 0, keepdims=False)
        steered = layer_rows == section_index
        steered_col = steered[:, None]
        normal_grad = lax.dot_general(
            lax.all_gather(grad_in, "row", axis=1, tiled=True),
            full_weight,
            contract,
            preferred_element_type=jnp.float32,
        )
        grad_float = grad_in.astype(jnp.float32)
        scaled = scaling * normal_grad
        plain_local = jnp.sum(unsteered * unsteered, -1)
        moved_local = jnp.sum(moved * moved, -1)
        scaled_plain = jnp.sum(scaled * unsteered, -1)
        scaled_moved = jnp.sum(scaled * moved, -1)
        plain_sq, moved_sq, curve_plain, curve_moved = lax.psum(
            (plain_local, moved_local, scaled_plain, scaled_moved), "row"
        )
        norm_plain = jnp.sqrt(plain_sq + epsilon)
        norm_moved = jnp.sqrt(moved_sq + epsilon)
        rescale = norm_plain / norm_moved
        square_sum = jnp.where(
            steered, norm_plain * norm_plain * moved_sq / (norm_moved * norm_moved), plain_sq
        )
        root_mean = jnp.sqrt(square_sum / D + epsilon)
        curvature = jnp.where(steered, rescale * curve_moved, curve_plain)
        rescaled = jnp.where(steered_col, moved * rescale[:, None], unsteered)
        factor = curvature / (D * root_mean**3)
        input_grad = grad_float + scaled / root_mean[:, None] - rescaled * factor[:, None]
        direction = moved / norm_moved[:, None]
        radial = lax.psum(jnp.sum(direction * input_grad, -1), "row")
        tangent = rescale[:, None] * (input_grad - direction * radial[:, None])
        below = jnp.where(
            steered_col, tangent + unsteered / norm_plain[:, None] * radial[:, None], input_grad
        )
        passed = jnp.where(active, below, 0.0).astype(jnp.bfloat16)
        results = jnp.where((slots == micro_index)[:, None, None], passed[None], results)
        steer_part = steer_part + jnp.sum(jnp.where(active & steered_col, tangent, 0.0), 0)
        if tick_index + 1 < ticks:
            received = passed_along(passed, "section", -1)
    steer_total = lax.psum(steer_part, ("section", "col"))
    return (results[None], steer_total / (MICRO * ROWS))


def solution(mesh):
    placed = (
        P("section", None, ("groups", "col"), "row"),
        P(None, ("groups", "col"), "row"),
        P("section", "row", "col"),
        P("section", "row"),
        P(("groups", "row")),
        P(None, ("groups", "col")),
    )
    return jax.shard_map(
        local,
        mesh=mesh,
        in_specs=placed,
        out_specs=(P("section", None, ("groups", "col"), "row"), P(("groups", "row"))),
        check_vma=False,
    )
```

profile of v0, /device:TPU:0, one launch (start us, length us, event | category | flops | bytes accessed | tf_op | source)
XLA Modules:
  0.0 1643.4 jit_solution(9179535473520483501)
XLA Ops:
  7.2 0.0 all-gather.11.cloned.1.call-start
  7.2 3.8 slice_select_fusion
  11.0 0.0 all-gather.11.cloned.1.call-update
  11.0 0.0 copy-start.5
  11.0 0.0 copy-start.7
  11.0 0.0 all-gather.13.cloned.1.call-start
  11.1 0.7 all-gather.13.cloned.1.call-update
  11.8 0.0 all-gather.7.cloned.1.call-start
  11.8 0.0 copy-done.5
  11.9 0.0 copy-done.7
  11.9 0.0 copy-start.8
  11.9 9.7 convert_element_type.29
  21.6 0.0 copy-done.8
  21.6 0.5 compare_reduce_fusion.2
  22.1 10.1 bitcast_add_fusion
  32.2 62.0 %all-gather.11.cloned.1.call-done = bf16[1,384,8192]{2,1,0:T(8,128)(2,1)} async-done(((bf16[1,384,4096]{2,1,0:T(8,128)(2,1)}), bf16[1,384,8192]{2,1,0:T(8,128)(2,1)}) %all-gather.11.cloned.1.call-update) | async-done | bytes 6291472 | tf_op jit(solution)/shard_map/all_gather | solution.py:52
  94.2 1112.3 %all-gather.13.cloned.1.call-done = bf16[1,4096,8192]{2,1,0:T(8,128)(2,1)} async-done(((bf16[1,4096,2048]{2,1,0:T(8,128)(2,1)}), bf16[1,4096,8192]{2,1,0:T(8,128)(2,1)}) %all-gather.13.cloned.1.call-update) | async-done | bytes 67108880 | tf_op jit(solution)/shard_map/all_gather | solution.py:31
  1206.5 36.6 %fusion.11 = (f32[384]{0:T(512)S(1)}, f32[384]{0:T(512)S(1)}, f32[384]{0:T(512)S(1)}, f32[384]{0:T(512)S(1)}, f32[384,4096]{1,0:T(8,128)}) fusion(f32[2,384,4096]{2,1,0:T(8,128)} %bitcast_add_fusion, s32[]{:T(128)S(6)} %min.12, f32[1,2,384,4096]{3,2,1,0:T(8,128)} %convert_element_type.29, bf16[1,4096,8192]{2,1,0:T(8,128)(2,1)} %all-gather.13.cloned.1.call-done, ...), kind=kOutput, calls=%fused_computation.17 | convolution fusion | flops 25783959552 | bytes 92297216 | tf_op jit(solution)/shard_map/dot_general | solution.py:51
  1243.1 5.0 all-reduce.2
  1248.1 11.2 multiply_reduce_fusion.2
  1259.3 4.9 psum.120
  1264.2 8.1 fusion.42
  1272.3 0.0 copy-start.2
  1272.3 1.7 copy-done.2
  1274.0 1.3 collective-permute-start
  1275.3 6.3 collective-permute-done
  1281.5 3.9 bitcast_select_fusion
  1285.5 0.0 all-gather.7.cloned.1.call-update
  1285.5 0.2 all-gather.9.cloned.1.call-start
  1285.7 0.0 copy-start.1
  1285.7 78.5 %all-gather.7.cloned.1.call-done = bf16[384,8192]{1,0:T(8,128)(2,1)} async-done(((bf16[384,4096]{1,0:T(8,128)(2,1)}), bf16[384,8192]{1,0:T(8,128)(2,1)}) %all-gather.7.cloned.1.call-update) | async-done | bytes 6291472 | tf_op jit(solution)/shard_map/all_gather | solution.py:52
  1364.2 36.7 %fusion.22 = (f32[384]{0:T(512)S(1)}, f32[384]{0:T(512)S(1)}, f32[384]{0:T(512)S(1)}, f32[384]{0:T(512)S(1)}, f32[384,4096]{1,0:T(8,128)}) fusion(f32[2,384,4096]{2,1,0:T(8,128)} %bitcast_add_fusion, s32[]{:T(128)S(6)} %min.11, f32[1,2,384,4096]{3,2,1,0:T(8,128)} %convert_element_type.29, bf16[384,8192]{1,0:T(8,128)(2,1)} %all-gather.7.cloned.1.call-done, ...), kind=kOutput, calls=%fused_computation.35 | convolution fusion | flops 25783959552 | bytes 92297216 | tf_op jit(solution)/shard_map/dot_general | solution.py:51
  1400.9 5.0 all-reduce.1
  1405.9 0.0 copy-done.1
  1405.9 10.5 multiply_reduce_fusion.1
  1416.4 4.9 psum.123
  1421.3 8.1 fusion.41
  1429.4 0.0 copy-start.4
  1429.4 1.6 copy-done.4
  1431.0 0.0 copy-start.6
  1431.0 1.4 collective-permute-start.1
  1432.4 6.3 collective-permute-done.1
  1438.7 1.8 broadcast_select_fusion
  1440.5 0.0 all-gather.9.cloned.1.call-update
  1440.6 0.0 copy-done.6
  1440.6 80.5 %all-gather.9.cloned.1.call-done = bf16[384,8192]{1,0:T(8,128)(2,1)} async-done(((bf16[384,4096]{1,0:T(8,128)(2,1)}), bf16[384,8192]{1,0:T(8,128)(2,1)}) %all-gather.9.cloned.1.call-update) | async-done | bytes 6291472 | tf_op jit(solution)/shard_map/all_gather | solution.py:52
  1521.1 36.6 %fusion.33 = (f32[384]{0:T(512)S(1)}, f32[384]{0:T(512)S(1)}, f32[384]{0:T(512)S(1)}, f32[384]{0:T(512)S(1)}, f32[384,4096]{1,0:T(8,128)}) fusion(f32[2,384,4096]{2,1,0:T(8,128)} %bitcast_add_fusion, s32[]{:T(128)S(6)} %min.10, f32[1,2,384,4096]{3,2,1,0:T(8,128)} %convert_element_type.29, bf16[384,8192]{1,0:T(8,128)(2,1)} %all-gather.9.cloned.1.call-done, ...), kind=kOutput, calls=%fused_computation.53 | convolution fusion | flops 25783959552 | bytes 92297216 | tf_op jit(solution)/shard_map/dot_general | solution.py:51
  1557.7 5.0 all-reduce
  1562.7 10.5 multiply_reduce_fusion
  1573.2 5.1 psum.126
  1578.3 0.0 copy-start
  1578.3 9.4 fusion.40
  1587.7 0.0 copy-done
  1587.7 0.0 copy-start.3
  1587.7 14.3 select_reduce_fusion.1
  1602.1 27.5 %psum.127 = f32[4096]{0:T(1024)S(1)} all-reduce(f32[4096]{0:T(1024)S(1)} %add_add_fusion), channel_id=1, replica_groups=mesh['groups'=2,'section'=2,'row'=2,'col'=4] {'section','col'}, use_global_device_ids=true, to_apply=%region_33.34 | all-reduce | flops 4096 | bytes 32768 | tf_op jit(solution)/shard_map/psum | solution.py:88
  1629.6 0.6 broadcast_multiply_fusion
  1630.2 0.0 copy-done.3
  1630.2 6.7 select_select_fusion
  (10 shorter events, 0.1 us)
Async XLA Ops:
  7.2 87.1 %all-gather.11.cloned.1.call-start = ((), (), s32[]{:S(2)}) async-start(), calls=%async_computation.2 | async-start | bytes 9437184 | tf_op jit(solution)/shard_map/all_gather | solution.py:52
  11.0 0.8 copy-start.5
  11.0 0.9 copy-start.7
  11.0 1195.5 %all-gather.13.cloned.1.call-start = ((), (), s32[]{:S(2)}) async-start(), calls=%async_computation.3 | async-start | bytes 83886080 | tf_op jit(solution)/shard_map/all_gather | solution.py:31
  11.8 1352.5 %all-gather.7.cloned.1.call-start = ((), (), s32[]{:S(2)}) async-start(), calls=%async_computation | async-start | bytes 9437184 | tf_op jit(solution)/shard_map/all_gather | solution.py:52
  11.9 9.7 copy-start.8
  1272.3 1.7 copy-start.2
  1274.0 7.5 collective-permute-start
  1285.5 235.6 %all-gather.9.cloned.1.call-start = ((), (), s32[]{:S(2)}) async-start(), calls=%async_computation.1 | async-start | bytes 9437184 | tf_op jit(solution)/shard_map/all_gather | solution.py:52
  1285.7 120.2 %copy-start.1 = (bf16[384,4096]{1,0:T(8,128)(2,1)S(1)}, bf16[384,4096]{1,0:T(8,128)(2,1)}, u32[]{:S(2)}) copy-start(bf16[384,4096]{1,0:T(8,128)(2,1)} %bitcast_select_fusion) | copy-start | bytes 9437188
  1429.4 1.6 copy-start.4
  1431.0 9.6 copy-start.6
  1431.0 7.7 collective-permute-start.1
  1578.3 9.4 copy-start
  1587.7 42.5 %copy-start.3 = (bf16[384,4096]{1,0:T(8,128)(2,1)S(1)}, bf16[384,4096]{1,0:T(8,128)(2,1)}, u32[]{:S(2)}) copy-start(bf16[384,4096]{1,0:T(8,128)(2,1)} %copy-done.2) | copy-start | bytes 9437188
Sparse Core Ops, SparseCore 0:
  11.1 83.0 all-gather.10
  95.8 1110.6 all-gather.12
  1285.6 78.5 all-gather.6
  1440.7 80.3 all-gather.8
where the time goes:
time: 1650 us; the launch traced here: 1640 us
  waiting for transfers between devices  1350 us (82%)
  matrix products  110 us (7%)
  other arithmetic  109 us (7%)
  blocking collectives  57.4 us (3%)
    all_gather x1, waiting for transfers between devices, local(): full_weight = lax.all_gather(local_weight, 'col', axis=1, tiled=True)  1110 us
    all_gather x3, waiting for transfers between devices, local(): lax.all_gather(grad_in, 'row', axis=1, tiled=True)  221 us
    dot_general x3, matrix products, local(): lax.dot_general(lax.all_gather(grad_in, 'row', axis=1, tiled=True), full_...  110 us
  transfers between devices with their start and end apart: 6, of which 6 were waited for; matrix products, arithmetic and copies ran while one was open for 1% of the time, Pallas kernels for 0%

commit v1 on v0

--- a/solution.py
+++ b/solution.py
@@ -28,7 +28,16 @@
     feature_count = unsteered_all.shape[2]
     local_weight = weights[0]
     contract = (((1,), (1,)), ((), ()))
-    full_weight = lax.all_gather(local_weight, "col", axis=1, tiled=True)
+
+    def regroup(full):
+        split = full.reshape(row_count, cols, groups, piece)
+        return jnp.swapaxes(split, 1, 2).reshape(row_count, cols * groups * piece)
+
+    groups = lax.axis_size("groups")
+    cols = lax.axis_size("col")
+    piece = local_weight.shape[1] // groups
+    own_piece = lax.dynamic_slice_in_dim(local_weight, lax.axis_index("groups") * piece, piece, 1)
+    full_weight = lax.all_gather(own_piece, ("groups", "col"), axis=1, tiled=True)
     ticks = MICRO + sections - 1
     received = jnp.zeros((row_count, feature_count), jnp.bfloat16)
     results = jnp.zeros((MICRO, row_count, feature_count), jnp.bfloat16)
@@ -49,7 +58,7 @@
         steered = layer_rows == section_index
         steered_col = steered[:, None]
         normal_grad = lax.dot_general(
-            lax.all_gather(grad_in, "row", axis=1, tiled=True),
+            regroup(lax.all_gather(grad_in, "row", axis=1, tiled=True)),
             full_weight,
             contract,
             preferred_element_type=jnp.float32,

time: 1650 us -> 1860 us (1.13)
  waiting for transfers between devices: 1350 us -> 1470 us
  local copies, waits for them, and re-layouts: 3.31 us -> 94.1 us
    all_gather x1, waiting for transfers between devices: 1110 us -> 1240 us  [local(): lax.all_gather(own_piece, ('groups', 'col'), axis=1, tiled=True)]
    reshape x0 -> x6, local copies, waits for them, and re-layouts: none -> 82.5 us  [regroup(): split = full.reshape(row_count, cols, groups, piece)]
  transfers between devices with their start and end apart: 6 -> 6, of which waited for: 6 -> 6; matrix products, arithmetic and copies ran while one was open for 1% -> 3% of each run, Pallas kernels for 0% -> 0%
where the time goes in v1:
time: 1860 us
  waiting for transfers between devices  1470 us (79%)
  matrix products  110 us (6%)
  other arithmetic  109 us (6%)
  local copies, waits for them, and re-layouts  94.1 us (5%)
  blocking collectives  57.1 us (3%)
    all_gather x1, waiting for transfers between devices, local(): lax.all_gather(own_piece, ('groups', 'col'), axis=1, tiled=True)  1240 us
    all_gather x3, waiting for transfers between devices, local(): lax.all_gather(grad_in, 'row', axis=1, tiled=True)  217 us
    dot_general x3, matrix products, local(): lax.dot_general(regroup(lax.all_gather(grad_in, 'row', axis=1, tiled=True...  110 us
    reshape x6, local copies, waits for them, and re-layouts, regroup(): split = full.reshape(row_count, cols, groups, piece)  82.5 us
  transfers between devices with their start and end apart: 6, of which 6 were waited for; matrix products, arithmetic and copies ran while one was open for 3% of the time, Pallas kernels for 0%

profile of v1, /device:TPU:0, one launch (start us, length us, event | category | flops | bytes accessed | tf_op | source)
XLA Modules:
  0.0 1857.7 jit_solution(14400749378231385533)
XLA Ops:
  7.2 0.0 all-gather.11.cloned.1.call-start
  7.2 3.8 slice_select_fusion
  11.0 0.0 all-gather.11.cloned.1.call-update
  11.0 0.0 all-gather.13.cloned.1.call-start
  11.1 7.7 constant_dynamic-slice_fusion
  18.7 0.0 all-gather.13.cloned.1.call-update
  18.7 0.0 all-gather.7.cloned.1.call-start
  18.8 0.6 copy-done.11
  19.5 0.0 copy-done.13
  19.5 0.0 copy-start.14
  19.5 10.7 convert_element_type.29
  30.2 0.0 copy-done.14
  30.2 0.6 compare_reduce_fusion.2
  30.8 9.0 bitcast_add_fusion
  39.8 54.4 %all-gather.11.cloned.1.call-done = bf16[1,384,8192]{2,1,0:T(8,128)(2,1)} async-done(((bf16[1,384,4096]{2,1,0:T(8,128)(2,1)}), bf16[1,384,8192]{2,1,0:T(8,128)(2,1)}) %all-gather.11.cloned.1.call-update) | async-done | bytes 6291472 | tf_op jit(solution)/shard_map/all_gather | solution.py:61
  94.2 11.2 reshape.112
  105.5 16.4 copy.8
  121.9 1240.8 %all-gather.13.cloned.1.call-done = bf16[1,4096,8192]{2,1,0:T(8,128)(2,1)} async-done(((bf16[1,4096,1024]{2,1,0:T(8,128)(2,1)}), bf16[1,4096,8192]{2,1,0:T(8,128)(2,1)}) %all-gather.13.cloned.1.call-update) | async-done | bytes 67108880 | tf_op jit(solution)/shard_map/all_gather | solution.py:40
  1362.7 36.7 %fusion.10 = (f32[384]{0:T(512)S(1)}, f32[384]{0:T(512)S(1)}, f32[384]{0:T(512)S(1)}, f32[384]{0:T(512)S(1)}, f32[384,4096]{1,0:T(8,128)}) fusion(f32[2,384,4096]{2,1,0:T(8,128)} %bitcast_add_fusion, s32[]{:T(128)S(6)} %min.12, f32[1,2,384,4096]{3,2,1,0:T(8,128)} %convert_element_type.29, bf16[384,8192]{0,1:T(8,128)(2,1)} %bitcast.166, ...), kind=kOutput, calls=%fused_computation.16 | convolution fusion | flops 25783959552 | bytes 92297216 | tf_op jit(solution)/shard_map/dot_general | solution.py:60
  1399.4 5.0 all-reduce.2
  1404.4 0.0 copy-start.5
  1404.4 0.0 copy-start.7
  1404.4 11.2 multiply_reduce_fusion.2
  1415.6 4.9 psum.120
  1420.5 0.0 copy-done.5
  1420.5 0.0 copy-done.7
  1420.5 8.1 fusion.41
  1428.7 0.0 copy-done.9
  1428.7 0.0 copy-start.2
  1428.7 1.7 copy-done.2
  1430.4 1.5 collective-permute-start
  1431.8 6.1 collective-permute-done
  1437.9 3.9 bitcast_select_fusion
  1441.8 0.0 all-gather.7.cloned.1.call-update
  1441.8 0.0 all-gather.9.cloned.1.call-start
  1441.9 81.7 %all-gather.7.cloned.1.call-done = bf16[384,8192]{1,0:T(8,128)(2,1)} async-done(((bf16[384,4096]{1,0:T(8,128)(2,1)}), bf16[384,8192]{1,0:T(8,128)(2,1)}) %all-gather.7.cloned.1.call-update) | async-done | bytes 6291472 | tf_op jit(solution)/shard_map/all_gather | solution.py:61
  1523.6 11.1 reshape.114
  1534.7 16.3 copy.9
  1551.1 36.9 %fusion.21 = (f32[384]{0:T(512)S(1)}, f32[384]{0:T(512)S(1)}, f32[384]{0:T(512)S(1)}, f32[384]{0:T(512)S(1)}, f32[384,4096]{1,0:T(8,128)}) fusion(f32[2,384,4096]{2,1,0:T(8,128)} %bitcast_add_fusion, s32[]{:T(128)S(6)} %min.11, f32[1,2,384,4096]{3,2,1,0:T(8,128)} %convert_element_type.29, bf16[384,8192]{0,1:T(8,128)(2,1)} %bitcast.168, ...), kind=kOutput, calls=%fused_computation.34 | convolution fusion | flops 25783959552 | bytes 92297216 | tf_op jit(solution)/shard_map/dot_general | solution.py:60
  1588.0 5.0 all-reduce.1
  1593.0 0.0 copy-done.1
  1593.0 10.4 multiply_reduce_fusion.1
  1603.4 4.9 psum.123
  1608.4 8.1 fusion.40
  1616.5 0.0 copy-start.4
  1616.5 1.6 copy-done.4
  1618.1 1.6 collective-permute-start.1
  1619.7 6.0 collective-permute-done.1
  1625.7 1.8 broadcast_select_fusion
  1627.6 0.0 all-gather.9.cloned.1.call-update
  1627.7 80.5 %all-gather.9.cloned.1.call-done = bf16[384,8192]{1,0:T(8,128)(2,1)} async-done(((bf16[384,4096]{1,0:T(8,128)(2,1)}), bf16[384,8192]{1,0:T(8,128)(2,1)}) %all-gather.9.cloned.1.call-update) | async-done | bytes 6291472 | tf_op jit(solution)/shard_map/all_gather | solution.py:61
  1708.1 11.1 reshape.116
  1719.3 16.2 copy.10
  1735.5 36.7 %fusion.32 = (f32[384]{0:T(512)S(1)}, f32[384]{0:T(512)S(1)}, f32[384]{0:T(512)S(1)}, f32[384]{0:T(512)S(1)}, f32[384,4096]{1,0:T(8,128)}) fusion(f32[2,384,4096]{2,1,0:T(8,128)} %bitcast_add_fusion, s32[]{:T(128)S(6)} %min.10, f32[1,2,384,4096]{3,2,1,0:T(8,128)} %convert_element_type.29, bf16[384,8192]{0,1:T(8,128)(2,1)} %bitcast.167, ...), kind=kOutput, calls=%fused_computation.52 | convolution fusion | flops 25783959552 | bytes 92297216 | tf_op jit(solution)/shard_map/dot_general | solution.py:60
  1772.2 5.0 all-reduce
  1777.2 10.5 multiply_reduce_fusion
  1787.7 4.9 psum.126
  1792.6 9.4 fusion.39
  1802.0 0.0 copy-done.10
  1802.0 0.0 copy-start.3
  1802.0 14.4 select_reduce_fusion.1
  1816.4 27.5 %psum.127 = f32[4096]{0:T(1024)S(1)} all-reduce(f32[4096]{0:T(1024)S(1)} %add_add_fusion), channel_id=1, replica_groups=mesh['groups'=2,'section'=2,'row'=2,'col'=4] {'section','col'}, use_global_device_ids=true, to_apply=%region_33.34 | all-reduce | flops 4096 | bytes 32768 | tf_op jit(solution)/shard_map/psum | solution.py:97
  1843.9 0.6 broadcast_multiply_fusion
  1844.5 6.7 select_select_fusion
  (25 shorter events, 0.2 us)
Async XLA Ops:
  7.2 87.1 %all-gather.11.cloned.1.call-start = ((), (), s32[]{:S(2)}) async-start(), calls=%async_computation.2 | async-start | bytes 9437184 | tf_op jit(solution)/shard_map/all_gather | solution.py:61
  11.0 1351.7 %all-gather.13.cloned.1.call-start = ((), (), s32[]{:S(2)}) async-start(), calls=%async_computation.3 | async-start | bytes 75497472 | tf_op jit(solution)/shard_map/all_gather | solution.py:40
  18.7 0.7 copy-start.11
  18.7 0.7 copy-start.13
  18.7 1504.8 %all-gather.7.cloned.1.call-start = ((), (), s32[]{:S(2)}) async-start(), calls=%async_computation | async-start | bytes 9437184 | tf_op jit(solution)/shard_map/all_gather | solution.py:61
  19.5 10.7 copy-start.14
  1404.4 16.1 copy-start.5
  1404.4 16.1 copy-start.7
  1420.5 8.1 copy-start.9
  1428.7 1.7 copy-start.2
  1430.4 7.5 collective-permute-start
  1441.8 266.3 %all-gather.9.cloned.1.call-start = ((), (), s32[]{:S(2)}) async-start(), calls=%async_computation.1 | async-start | bytes 9437184 | tf_op jit(solution)/shard_map/all_gather | solution.py:61
  1551.1 41.9 %copy-start.1 = (bf16[384,4096]{1,0:T(8,128)(2,1)S(1)}, bf16[384,4096]{1,0:T(8,128)(2,1)}, u32[]{:S(2)}) copy-start(bf16[384,4096]{1,0:T(8,128)(2,1)} %bitcast_select_fusion) | copy-start | bytes 9437188
  1616.5 1.6 copy-start.4
  1618.1 9.6 copy-start.12
  1618.1 7.7 collective-permute-start.1
  1792.6 9.4 copy-start
  1792.6 9.4 copy-start.6
  1792.6 9.4 copy-start.8
  1792.6 9.4 copy-start.10
  1802.0 42.5 %copy-start.3 = (bf16[384,4096]{1,0:T(8,128)(2,1)S(1)}, bf16[384,4096]{1,0:T(8,128)(2,1)}, u32[]{:S(2)}) copy-start(bf16[384,4096]{1,0:T(8,128)(2,1)} %copy-done.2) | copy-start | bytes 9437188
Sparse Core Ops, SparseCore 0:
  11.1 83.0 all-gather.10
  95.8 1266.8 all-gather.12
  1441.9 81.5 all-gather.6
  1627.7 80.3 all-gather.8

commit v2 on v0

v2 whole, which is shorter than its diff:
```python
import jax
import jax.numpy as jnp
from jax import lax
from jax.sharding import PartitionSpec as P

D = 8192
ROWS = 1536
MICRO = 2


epsilon = 1e-06


def shifted(value, axis, steps=1):
    count = lax.axis_size(axis)
    return lax.ppermute(value, axis, [(source, (source + steps) % count) for source in range(count)])


def columns(value, start, width):
    return lax.dynamic_slice_in_dim(value, start, width, value.ndim - 1)


def after(value, earlier):
    return lax.optimization_barrier((value, earlier))[0]


def local(hidden, upstream, weights, norm_gains, steering, steer_layer):
    core = lax.axis_index("section")
    row_index = lax.axis_index("row")
    col_index = lax.axis_index("col")
    group = lax.axis_index("groups")
    row_devices = lax.axis_size("row")
    cols = lax.axis_size("col")
    groups = lax.axis_size("groups")
    micro, row_count, features = upstream.shape
    tokens = micro * row_count
    half = features // 2
    depth = weights.shape[2]
    part = depth // groups
    f32 = jnp.float32

    def own_columns(value):
        return columns(value, core * half, half)

    def per_section(mine, received):
        return jnp.where(core == 0, mine, received), jnp.where(core == 1, mine, received)

    def over_cores(value, axis):
        mine = lax.dynamic_slice_in_dim(value, core * half, half, axis)
        given = lax.dynamic_slice_in_dim(value, (1 - core) * half, half, axis)
        return per_section(mine, shifted(given, "section"))

    weight_of = over_cores(weights[0], 0)
    hidden_of = over_cores(hidden[0].reshape(tokens, features), 1)
    gain_of = over_cores(norm_gains[0], 0)
    steer_vec = own_columns(steering).astype(f32)
    layers = steer_layer.reshape(tokens)
    upstream_rows = upstream.reshape(tokens, features)

    earlier, sent = [], []
    pieces = {}
    for section, count in ((1, 2), (0, 4)):
        count = max(1, min(count, part // 128))
        width = part // count
        held = []
        for chunk in range(count):
            own = columns(weight_of[section], group * part + chunk * width, width)
            own = after(own, tuple(earlier))
            gathered = lax.all_gather(own, "col", axis=1, tiled=True)
            others = jnp.concatenate(
                [columns(gathered, ((col_index + step) % cols) * width, width) for step in range(1, cols)], 1
            )
            held.append((others, shifted(others, "groups")))
            earlier = [others] + [held_before[1] for held_before in sent[-1:]]
            sent.append(held[-1])
        pieces[section] = (width, held)

    def projected(full, section):
        width, held = pieces[section]

        def times(left, right):
            return lax.dot_general(left, right, (((1,), (1,)), ((), ())), preferred_element_type=f32)

        total = times(columns(full, col_index * depth, depth), weight_of[section])
        for chunk, sides in enumerate(held):
            for side, block in enumerate(sides):
                owner = (group + side) % groups
                start = owner * part + chunk * width
                left = jnp.concatenate(
                    [columns(full, ((col_index + step) % cols) * depth + start, width) for step in range(1, cols)], 1
                )
                total = total + times(left, block)
        return total

    def all_features(own):
        if row_devices == 2:
            other = shifted(own, "row")
            both = jnp.concatenate([jnp.where(row_index == 0, own, other), jnp.where(row_index == 0, other, own)], 1)
            if own.shape[1] == features:
                return both
            there = shifted(both, "section")
            lower = jnp.where(core == 0, both, there)
            upper = jnp.where(core == 0, there, both)
            return jnp.concatenate([lower[:, :half], upper[:, :half], lower[:, half:], upper[:, half:]], 1)
        if own.shape[1] == features:
            return lax.all_gather(own, "row", axis=1, tiled=True)
        return lax.all_gather(own, ("row", "section"), axis=1, tiled=True)

    local_sums = []
    for section in range(2):
        unsteered = hidden_of[section].astype(f32)
        moved = unsteered + steer_vec
        local_sums += [jnp.sum(unsteered * unsteered, -1), jnp.sum(moved * moved, -1)]
    sums = lax.psum(tuple(local_sums), ("row", "section"))

    incoming = own_columns(upstream_rows)
    full = all_features(upstream_rows)
    steer_part = jnp.zeros((half,), f32)
    blocks = [None, None]
    for section in (1, 0):
        plain_sq, moved_sq = sums[2 * section], sums[2 * section + 1]
        steered = layers == section
        steered_col = steered[:, None]
        unsteered = hidden_of[section].astype(f32)
        moved = unsteered + steer_vec
        grad_float = incoming.astype(f32)
        scaled = gain_of[section].astype(f32) * projected(full, section)
        chosen = jnp.where(steered_col, moved, unsteered)
        curve, inner = lax.psum(
            (jnp.sum(scaled * chosen, -1), jnp.sum(grad_float * moved, -1)), ("row", "section")
        )
        norm_plain = jnp.sqrt(plain_sq + epsilon)
        norm_moved = jnp.sqrt(moved_sq + epsilon)
        rescale = norm_plain / norm_moved
        square_sum = jnp.where(
            steered, norm_plain * norm_plain * moved_sq / (norm_moved * norm_moved), plain_sq
        )
        root_mean = jnp.sqrt(square_sum / D + epsilon)
        scale = jnp.where(steered, rescale, 1.0)
        factor = scale * curve / (D * root_mean**3)
        input_grad = grad_float + scaled / root_mean[:, None] - chosen * (scale * factor)[:, None]
        radial = (inner + curve / root_mean - rescale * factor * moved_sq) / norm_moved
        tangent = rescale[:, None] * (input_grad - moved * (radial / norm_moved)[:, None])
        below = jnp.where(steered_col, tangent + unsteered * (radial / norm_plain)[:, None], input_grad)
        passed = below.astype(jnp.bfloat16)
        blocks[section] = passed
        steer_part = steer_part + jnp.sum(jnp.where(steered_col, tangent, 0.0), 0)
        if section == 1:
            incoming = passed
            full = all_features(passed)
    kept = jnp.where(core == 0, blocks[0], blocks[1])
    received = shifted(jnp.where(core == 0, blocks[1], blocks[0]), "section")
    lower = jnp.where(core == 0, kept, received)
    upper = jnp.where(core == 0, received, kept)
    result = jnp.concatenate([lower, upper], 1).reshape(1, micro, row_count, features)
    slots = jnp.where(jnp.arange(2)[:, None] == core, steer_part[None], 0.0).reshape(features)
    steer_total = lax.psum(slots, ("section", "col"))
    return (result, steer_total / (MICRO * ROWS))


def solution(mesh):
    placed = (
        P("section", None, ("groups", "col"), "row"),
        P(None, ("groups", "col"), "row"),
        P("section", "row", "col"),
        P("section", "row"),
        P(("groups", "row")),
        P(None, ("groups", "col")),
    )
    return jax.shard_map(
        local,
        mesh=mesh,
        in_specs=placed,
        out_specs=(P("section", None, ("groups", "col"), "row"), P(("groups", "row"))),
        check_vma=False,
    )
```

time: 1650 us -> 954 us (0.58)
  waiting for transfers between devices: 1350 us -> 602 us
  local copies, waits for them, and re-layouts: 3.31 us -> 52.8 us
  other arithmetic: 109 us -> 84.9 us
  matrix products: 110 us -> 132 us
    all_gather x4 -> x6, waiting for transfers between devices: 1330 us -> 432 us  [local(): gathered = lax.all_gather(own, 'col', axis=1, tiled=True)]
    ppermute x2 -> x13, waiting for transfers between devices: 12.5 us -> 170 us  [shifted(): lax.ppermute(value, axis, [(source, (source + steps) % count) for source...]
    dynamic_slice x0 -> x13, local copies, waits for them, and re-layouts: none -> 38.3 us  [the longest x10 25.7 us: columns(): return lax.dynamic_slice_in_dim(value, start, width, value.ndim - 1)]
    reduce_sum x4 -> x1, other arithmetic: 46.4 us -> 9.18 us  [local(): steer_part = steer_part + jnp.sum(jnp.where(steered_col, tangent, 0.0), 0)]
    concatenate x0 -> x11, other arithmetic: none -> 32.1 us  [the longest x6 13.2 us: local(): jnp.concatenate([columns(gathered, (col_index + step) % cols * width, wid...]
    convert_element_type x5 -> x3, other arithmetic: 35.2 us -> 9.17 us  [the longest x1 8.56 us: local(): passed = below.astype(jnp.bfloat16)]
    dot_general x3 -> x14, matrix products: 110 us -> 132 us  [times(): lax.dot_general(left, right, (((1,), (1,)), ((), ())), preferred_element_...]
    select_n x4 -> x6, other arithmetic: 16.2 us -> 33.7 us  [the longest x1 10.9 us: per_section(): jnp.where(core == 0, mine, received)]
  transfers between devices with their start and end apart: 6 -> 19, of which waited for: 6 -> 12; matrix products, arithmetic and copies ran while one was open for 1% -> 20% of each run, Pallas kernels for 0% -> 0%
where the time goes in v2:
time: 954 us; the launch traced here: 949 us
  waiting for transfers between devices  602 us (63%)
  matrix products  132 us (14%)
  other arithmetic  84.9 us (9%)
  local copies, waits for them, and re-layouts  52.8 us (6%)
  blocking collectives  47.8 us (5%)
  between operations  15.4 us (2%)
  starting transfers between devices  13.5 us (1%)
    all_gather x6, waiting for transfers between devices, local(): gathered = lax.all_gather(own, 'col', axis=1, tiled=True)  432 us
    ppermute x13, waiting for transfers between devices, shifted(): lax.ppermute(value, axis, [(source, (source + steps) % count) for source...  170 us
    dot_general x14, matrix products, times(): lax.dot_general(left, right, (((1,), (1,)), ((), ())), preferred_element_...  132 us
    psum x1, blocking collectives, local(): steer_total = lax.psum(slots, ('section', 'col'))  26.2 us
    dynamic_slice x10, local copies, waits for them, and re-layouts, columns(): return lax.dynamic_slice_in_dim(value, start, width, value.ndim - 1)  25.7 us
    psum x2, blocking collectives, local(): sums = lax.psum(tuple(local_sums), ('row', 'section'))  21.6 us
  transfers between devices with their start and end apart: 19, of which 12 were waited for; matrix products, arithmetic and copies ran while one was open for 20% of the time, Pallas kernels for 0%

profile of v2, /device:TPU:0, one launch (start us, length us, event | category | flops | bytes accessed | tf_op | source)
XLA Modules:
  0.0 948.9 jit_solution(9540343544707476704)
XLA Ops:
  7.2 8.3 dynamic-slice_bitcast_fusion
  16.0 13.1 %collective-permute-done.3 = bf16[2048,2048]{1,0:T(8,128)(2,1)} collective-permute-done((bf16[2048,2048]{1,0:T(8,128)(2,1)}, bf16[2048,2048]{1,0:T(8,128)(2,1)}, u32[]{:S(2)}, u32[]{:S(2)}) %collective-permute-start.3) | collective-permute-done | bytes 8388640 | tf_op jit(solution)/shard_map/ppermute | solution.py:16
  29.1 10.9 %bitcast_select_fusion = (bf16[2048,2048]{1,0:T(8,128)(2,1)}, bf16[2048,2048]{1,0:T(8,128)(2,1)S(1)}) fusion(bf16[2048,2048]{1,0:T(8,128)(2,1)} %collective-permute-done.3, pred[]{:T(512)S(6)} %eq.126, bf16[1,4096,2048]{2,1,0:T(8,128)(2,1)} %param.8, s32[]{:T(128)S(6)} %select_n.422, pred[]{:T(512)S(6)} %eq.133), kind=kLoop, calls=%fused_computation.41 | loop fusion | flops 8388608 | bytes 33554440 | tf_op jit(solution)/shard_map/jit(_where)/select_n | solution.py:46
  40.0 3.3 copy-done.4
  43.3 2.5 constant_dynamic-slice_fusion.47
  46.0 152.3 %all-gather.7.cloned.1.call-done = bf16[2048,2048]{1,0:T(8,128)(2,1)} async-done(((bf16[2048,512]{1,0:T(8,128)(2,1)}), bf16[2048,2048]{1,0:T(8,128)(2,1)}) %all-gather.7.cloned.1.call-update) | async-done | bytes 8388624 | tf_op jit(solution)/shard_map/all_gather | solution.py:69
  198.3 3.3 constant_dynamic-slice_fusion.46
  201.6 3.8 pad_maximum_fusion.1
  205.7 1.5 collective-permute-start.4
  208.8 4.2 constant_dynamic-slice_fusion.50
  214.4 4.7 constant_dynamic-slice_fusion.36
  219.1 134.6 %all-gather.9.cloned.1.call-done = bf16[2048,2048]{1,0:T(8,128)(2,1)} async-done(((bf16[2048,512]{1,0:T(8,128)(2,1)}), bf16[2048,2048]{1,0:T(8,128)(2,1)}) %all-gather.9.cloned.1.call-update) | async-done | bytes 8388624 | tf_op jit(solution)/shard_map/all_gather | solution.py:69
  353.6 3.3 constant_dynamic-slice_fusion.42
  356.9 3.7 pad_maximum_fusion.2
  363.4 5.6 broadcast_select_fusion.2
  369.0 3.8 fusion.121
  372.7 3.8 fusion.122
  376.6 11.2 %fusion.31 = f32[768,2048]{1,0:T(8,128)} fusion(bf16[2048,2048]{1,0:T(8,128)(2,1)} %copy-done.4, s32[]{:T(128)S(6)} %select_n.432, bf16[768,4096]{1,0:T(8,128)(2,1)S(1)} %get-tuple-element.88, bf16[768,4096]{1,0:T(8,128)(2,1)S(1)} %get-tuple-element.87), kind=kOutput, calls=%fused_computation.83 | convolution fusion | flops 6448742400 | bytes 27262980 | tf_op jit(solution)/shard_map/dot_general | solution.py:82
  387.8 9.5 fusion.35
  397.3 10.6 %fusion.41 = f32[768,2048]{1,0:T(8,128)} fusion(bf16[2048,1536]{1,0:T(8,128)(2,1)} %collective-permute-done.4, bf16[768,512]{1,0:T(8,128)(2,1)S(1)} %copy-done.36, bf16[768,512]{1,0:T(8,128)(2,1)S(1)} %copy-done.35, bf16[768,512]{1,0:T(8,128)(2,1)S(1)} %copy-done.34), kind=kOutput, calls=%fused_computation.104 | convolution fusion | flops 4838916096 | bytes 14942208 | tf_op jit(solution)/shard_map/dot_general | solution.py:82
  408.0 7.7 fusion.47
  415.7 25.3 %all-gather.11.cloned.1.call-done = bf16[2048,1024]{1,0:T(8,128)(2,1)} async-done(((bf16[2048,256]{1,0:T(8,128)(2,1)}), bf16[2048,1024]{1,0:T(8,128)(2,1)}) %all-gather.11.cloned.1.call-update) | async-done | bytes 4194320 | tf_op jit(solution)/shard_map/all_gather | solution.py:69
  441.0 2.1 constant_dynamic-slice_fusion.35
  444.1 1.7 pad_maximum_fusion.5
  447.3 52.9 %collective-permute-done.5 = bf16[2048,1536]{1,0:T(8,128)(2,1)} collective-permute-done((bf16[2048,1536]{1,0:T(8,128)(2,1)}, bf16[2048,1536]{1,0:T(8,128)(2,1)}, u32[]{:S(2)}, u32[]{:S(2)}) %collective-permute-start.5) | collective-permute-done | bytes 6291488 | tf_op jit(solution)/shard_map/ppermute | solution.py:16
  500.3 20.6 %fusion.23 = (f32[768]{0:T(1024)S(1)}, f32[768]{0:T(1024)S(1)}, f32[768]{0:T(1024)S(1)}, f32[768]{0:T(1024)S(1)}, bf16[768,2048]{1,0:T(8,128)(2,1)}, /*index=5*/f32[768,2048]{1,0:T(8,128)}) fusion(f32[2048]{0:T(1024)S(1)} %dynamic-slice_convert_fusion, bf16[768,4096]{1,0:T(8,128)(2,1)} %bitcast.24, s32[]{:T(128)S(6)} %select_n.422, ...), kind=kOutput, calls=%fused_computation.63 | convolution fusion | flops 4867224576 | bytes 52720388 | tf_op jit(solution)/shard_map/dot_general | solution.py:82
  520.9 10.9 %all-reduce.1 = (f32[768]{0:T(1024)S(1)}, f32[768]{0:T(1024)S(1)}, f32[768]{0:T(1024)S(1)}, f32[768]{0:T(1024)S(1)}) all-reduce(f32[768]{0:T(1024)S(1)} %get-tuple-element.19, f32[768]{0:T(1024)S(1)} %get-tuple-element.16, f32[768]{0:T(1024)S(1)} %get-tuple-element.17, ...), channel_id=1, replica_groups=mesh['groups'=2,'section'=2,'row'=2,'col'=4] {'row','section'}, use_global_device_ids=true, to_apply=%region_5.6 | all-reduce | flops 3072 | bytes 24576 | tf_op jit(solution)/shard_map/psum | solution.py:114
  531.9 8.6 fusion.29
  541.9 37.3 %all-gather.13.cloned.1.call-done = bf16[2048,1024]{1,0:T(8,128)(2,1)} async-done(((bf16[2048,256]{1,0:T(8,128)(2,1)}), bf16[2048,1024]{1,0:T(8,128)(2,1)}) %all-gather.13.cloned.1.call-update) | async-done | bytes 4194320 | tf_op jit(solution)/shard_map/all_gather | solution.py:69
  579.2 2.1 constant_dynamic-slice_fusion.25
  582.2 1.7 pad_maximum_fusion.6
  584.1 25.7 %collective-permute-done.6 = bf16[768,2048]{1,0:T(8,128)(2,1)} collective-permute-done((bf16[768,2048]{1,0:T(8,128)(2,1)S(1)}, bf16[768,2048]{1,0:T(8,128)(2,1)}, u32[]{:S(2)}, u32[]{:S(2)}) %collective-permute-start.6) | collective-permute-done | bytes 3145760 | tf_op jit(solution)/shard_map/ppermute | solution.py:16
  609.8 2.3 broadcast_select_fusion.5
  612.2 3.9 pad_maximum_fusion.3
  616.8 1.5 collective-permute-start.9
  618.3 44.7 %all-gather.15.cloned.1.call-done = bf16[2048,1024]{1,0:T(8,128)(2,1)} async-done(((bf16[2048,256]{1,0:T(8,128)(2,1)}), bf16[2048,1024]{1,0:T(8,128)(2,1)}) %all-gather.15.cloned.1.call-update) | async-done | bytes 4194320 | tf_op jit(solution)/shard_map/all_gather | solution.py:69
  662.9 2.1 constant_dynamic-slice_fusion.15
  666.0 1.9 pad_maximum_fusion.7
  667.9 19.7 %collective-permute-done.9 = bf16[2048,768]{1,0:T(8,128)(2,1)} collective-permute-done((bf16[2048,768]{1,0:T(8,128)(2,1)}, bf16[2048,768]{1,0:T(8,128)(2,1)}, u32[]{:S(2)}, u32[]{:S(2)}) %collective-permute-start.9) | collective-permute-done | bytes 3145760 | tf_op jit(solution)/shard_map/ppermute | solution.py:16
  687.8 6.7 broadcast_select_fusion.1
  695.7 2.5 fusion.152
  698.2 3.9 pad_maximum_fusion
  702.4 3.1 constant_dynamic-slice_fusion.2
  705.6 2.8 copy-done
  708.3 6.5 fusion.67
  714.8 6.5 fusion.79
  722.8 4.6 fusion.61
  727.4 38.2 %all-gather.17.cloned.1.call-done = bf16[2048,1024]{1,0:T(8,128)(2,1)} async-done(((bf16[2048,256]{1,0:T(8,128)(2,1)}), bf16[2048,1024]{1,0:T(8,128)(2,1)}) %all-gather.17.cloned.1.call-update) | async-done | bytes 4194320 | tf_op jit(solution)/shard_map/all_gather | solution.py:69
  765.6 2.3 constant_dynamic-slice_fusion.5
  768.2 1.5 collective-permute-start.11
  769.7 4.6 fusion.73
  774.4 10.1 %fusion.33 = f32[768,2048]{1,0:T(8,128)} fusion(bf16[2048,2048]{1,0:T(8,128)(2,1)S(1)} %bitcast.22, bf16[768,8192]{1,0:T(8,128)(2,1)} %copy-done, s32[]{:T(128)S(6)} %select_n.432), kind=kOutput, calls=%fused_computation.88 | convolution fusion | flops 6442450944 | bytes 17825796 | tf_op jit(solution)/shard_map/dot_general | solution.py:82
  784.6 4.8 fusion.85
  789.4 3.3 collective-permute-done.10
  792.7 6.6 fusion.91
  799.3 4.6 fusion.97
  803.9 54.8 %collective-permute-done.11 = bf16[2048,768]{1,0:T(8,128)(2,1)} collective-permute-done((bf16[2048,768]{1,0:T(8,128)(2,1)S(1)}, bf16[2048,768]{1,0:T(8,128)(2,1)}, u32[]{:S(2)}, u32[]{:S(2)}) %collective-permute-start.11) | collective-permute-done | bytes 3145760 | tf_op jit(solution)/shard_map/ppermute | solution.py:16
  858.7 24.5 %fusion.15 = (f32[768]{0:T(1024)}, f32[768]{0:T(1024)}, f32[768]{0:T(1024)}, f32[768]{0:T(1024)}, bf16[768,2048]{1,0:T(8,128)(2,1)}, /*index=5*/f32[768,2048]{1,0:T(8,128)}) fusion(bf16[768,2048]{1,0:T(8,128)(2,1)S(1)} %get-tuple-element.40, f32[2048]{0:T(1024)S(1)} %dynamic-slice_convert_fusion, pred[768]{0:T(1024)(128)(4,1)S(1)} %eq.129, ...), kind=kOutput, calls=%fused_computation.55 | convolution fusion | flops 2454057984 | bytes 73560840 | tf_op jit(solution)/shard_map/dot_general | solution.py:82
  883.3 10.7 %all-reduce = (f32[768]{0:T(1024)S(1)}, f32[768]{0:T(1024)S(1)}, f32[768]{0:T(1024)S(1)}, f32[768]{0:T(1024)S(1)}) all-reduce(f32[768]{0:T(1024)} %get-tuple-element.18, f32[768]{0:T(1024)} %get-tuple-element.13, f32[768]{0:T(1024)} %get-tuple-element.14, ...), channel_id=1, replica_groups=mesh['groups'=2,'section'=2,'row'=2,'col'=4] {'row','section'}, use_global_device_ids=true, to_apply=%region_1.2 | all-reduce | flops 3072 | bytes 24576 | tf_op jit(solution)/shard_map/psum | solution.py:114
  894.1 9.2 select_reduce_fusion
  903.3 4.7 broadcast_select_fusion.9
  908.1 26.2 %psum.71 = f32[4096]{0:T(1024)S(1)} all-reduce(f32[4096]{0:T(1024)S(1)} %bitcast.30), channel_id=1, replica_groups=mesh['groups'=2,'section'=2,'row'=2,'col'=4] {'section','col'}, use_global_device_ids=true, to_apply=%region_18.19 | all-reduce | flops 4096 | bytes 32768 | tf_op jit(solution)/shard_map/psum | solution.py:157
  934.9 3.4 broadcast_select_fusion.8
  938.3 3.5 pad_maximum_fusion.4
  (159 shorter events, 17.0 us)
Async XLA Ops:
  7.2 191.1 %all-gather.7.cloned.1.call-start = ((), (), s32[]{:S(2)}) async-start(), calls=%async_computation | async-start | bytes 10485760 | tf_op jit(solution)/shard_map/all_gather | solution.py:69
  15.5 13.6 %collective-permute-start.3 = (bf16[2048,2048]{1,0:T(8,128)(2,1)}, bf16[2048,2048]{1,0:T(8,128)(2,1)}, u32[]{:S(2)}, u32[]{:S(2)}) collective-permute-start(bf16[2048,2048]{1,0:T(8,128)(2,1)} %dynamic-slice_bitcast_fusion), channel_id=1, source_target_pairs={{0,8},{8,0},{1,9},{9,1},{2,10},{10,2},{3,11},{11,3},{4,12},{12,4},... | collective-permute-start | bytes 25165832 | tf_op jit(solution)/shard_map/ppermute | solution.py:16
  45.9 307.7 %all-gather.9.cloned.1.call-start = ((), (), s32[]{:S(2)}) async-start(), calls=%async_computation.1 | async-start | bytes 10485760 | tf_op jit(solution)/shard_map/all_gather | solution.py:69
  201.6 4.0 copy-start.6
  201.6 7.1 copy-start.51
  205.6 7.9 copy-start.53
  205.6 7.9 copy-start.52
  205.6 235.4 %all-gather.11.cloned.1.call-start = ((), (), s32[]{:S(2)}) async-start(), calls=%async_computation.2 | async-start | bytes 5242880 | tf_op jit(solution)/shard_map/all_gather | solution.py:69
  205.7 157.3 %collective-permute-start.4 = (bf16[2048,1536]{1,0:T(8,128)(2,1)}, bf16[2048,1536]{1,0:T(8,128)(2,1)}, u32[]{:S(2)}, u32[]{:S(2)}) collective-permute-start(bf16[2048,1536]{1,0:T(8,128)(2,1)} %pad_maximum_fusion.1), channel_id=1, source_target_pairs={{0,16},{16,0},{1,17},{17,1},{2,18},{18,2},{3,19},{19,3},{4,20},{20... | collective-permute-start | bytes 18874376 | tf_op jit(solution)/shard_map/ppermute | solution.py:16
  207.2 156.1 %collective-permute-start.2 = (bf16[768,4096]{1,0:T(8,128)(2,1)}, bf16[768,4096]{1,0:T(8,128)(2,1)}, u32[]{:S(2)}, u32[]{:S(2)}) collective-permute-start(bf16[768,4096]{1,0:T(8,128)(2,1)} %bitcast.23), channel_id=1, source_target_pairs={{0,4},{4,0},{1,5},{5,1},{2,6},{6,2},{3,7},{7,3},{8,12},{12,8},{9,1... | collective-permute-start | bytes 18874376 | tf_op jit(solution)/shard_map/ppermute | solution.py:16
  208.8 5.0 collective-permute-start.1
  213.0 287.3 %collective-permute-start = (bf16[768,2048]{1,0:T(8,128)(2,1)}, bf16[768,2048]{1,0:T(8,128)(2,1)}, u32[]{:S(2)}, u32[]{:S(2)}) collective-permute-start(bf16[768,2048]{1,0:T(8,128)(2,1)} %constant_dynamic-slice_fusion.50), channel_id=1, source_target_pairs={{0,8},{8,0},{1,9},{9,1},{2,10},{10,2},{3,11},{11,3},{4,12},{12,4},... | collective-permute-start | bytes 9437192 | tf_op jit(solution)/shard_map/ppermute | solution.py:16
  213.7 318.2 %copy-start.50 = (pred[768]{0:T(1024)(128)(4,1)}, pred[768]{0:T(1024)(128)(4,1)S(1)}, u32[]{:S(2)}) copy-start(pred[768]{0:T(1024)(128)(4,1)S(1)} %eq.132) | copy-start | bytes 2308
  356.9 4.0 copy-start.9
  356.9 4.6 copy-start.11
  361.5 138.7 %collective-permute-start.5 = (bf16[2048,1536]{1,0:T(8,128)(2,1)}, bf16[2048,1536]{1,0:T(8,128)(2,1)}, u32[]{:S(2)}, u32[]{:S(2)}) collective-permute-start(bf16[2048,1536]{1,0:T(8,128)(2,1)} %pad_maximum_fusion.2), channel_id=1, source_target_pairs={{0,16},{16,0},{1,17},{17,1},{2,18},{18,2},{3,19},{19,3},{4,20},{20... | collective-permute-start | bytes 18874376 | tf_op jit(solution)/shard_map/ppermute | solution.py:16
  363.0 216.2 %all-gather.13.cloned.1.call-start = ((), (), s32[]{:S(2)}) async-start(), calls=%async_computation.3 | async-start | bytes 5242880 | tf_op jit(solution)/shard_map/all_gather | solution.py:69
  387.8 9.5 %copy-start.34 = (bf16[768,512]{1,0:T(8,128)(2,1)S(1)}, bf16[768,512]{1,0:T(8,128)(2,1)}, u32[]{:S(2)}) copy-start(bf16[768,512]{1,0:T(8,128)(2,1)} %get-tuple-element.79) | copy-start | bytes 2359300
  387.8 9.5 %copy-start.35 = (bf16[768,512]{1,0:T(8,128)(2,1)S(1)}, bf16[768,512]{1,0:T(8,128)(2,1)}, u32[]{:S(2)}) copy-start(bf16[768,512]{1,0:T(8,128)(2,1)} %get-tuple-element.80) | copy-start | bytes 2359300
  387.8 9.5 %copy-start.36 = (bf16[768,512]{1,0:T(8,128)(2,1)S(1)}, bf16[768,512]{1,0:T(8,128)(2,1)}, u32[]{:S(2)}) copy-start(bf16[768,512]{1,0:T(8,128)(2,1)} %get-tuple-element.82) | copy-start | bytes 2359300
  397.3 10.7 %copy-start.8 = (bf16[2048,512]{1,0:T(8,128)(2,1)S(1)}, bf16[2048,512]{1,0:T(8,128)(2,1)}, u32[]{:S(2)}) copy-start(bf16[2048,512]{1,0:T(8,128)(2,1)} %copy-done.7) | copy-start | bytes 6291460
  397.3 10.7 %copy-start.10 = (bf16[2048,512]{1,0:T(8,128)(2,1)S(1)}, bf16[2048,512]{1,0:T(8,128)(2,1)}, u32[]{:S(2)}) copy-start(bf16[2048,512]{1,0:T(8,128)(2,1)} %copy-done.9) | copy-start | bytes 6291460
  397.3 10.7 %copy-start.12 = (bf16[2048,512]{1,0:T(8,128)(2,1)S(1)}, bf16[2048,512]{1,0:T(8,128)(2,1)}, u32[]{:S(2)}) copy-start(bf16[2048,512]{1,0:T(8,128)(2,1)} %copy-done.11) | copy-start | bytes 6291460
  397.3 10.7 %copy-start.33 = (bf16[768,512]{1,0:T(8,128)(2,1)S(1)}, bf16[768,512]{1,0:T(8,128)(2,1)}, u32[]{:S(2)}) copy-start(bf16[768,512]{1,0:T(8,128)(2,1)} %get-tuple-element.85) | copy-start | bytes 2359300
  415.7 84.6 %copy-start.31 = (bf16[768,512]{1,0:T(8,128)(2,1)S(1)}, bf16[768,512]{1,0:T(8,128)(2,1)}, u32[]{:S(2)}) copy-start(bf16[768,512]{1,0:T(8,128)(2,1)} %get-tuple-element.81) | copy-start | bytes 2359300
  415.7 84.6 %copy-start.32 = (bf16[768,512]{1,0:T(8,128)(2,1)S(1)}, bf16[768,512]{1,0:T(8,128)(2,1)}, u32[]{:S(2)}) copy-start(bf16[768,512]{1,0:T(8,128)(2,1)} %get-tuple-element.86) | copy-start | bytes 2359300
  443.1 4.1 copy-start.17
  445.8 138.2 %collective-permute-start.8 = (bf16[2048,768]{1,0:T(8,128)(2,1)}, bf16[2048,768]{1,0:T(8,128)(2,1)}, u32[]{:S(2)}, u32[]{:S(2)}) collective-permute-start(bf16[2048,768]{1,0:T(8,128)(2,1)} %pad_maximum_fusion.5), channel_id=1, source_target_pairs={{0,16},{16,0},{1,17},{17,1},{2,18},{18,2},{3,19},{19,3},{4,20},{20... | collective-permute-start | bytes 9437192 | tf_op jit(solution)/shard_map/ppermute | solution.py:16
  500.2 162.7 %all-gather.15.cloned.1.call-start = ((), (), s32[]{:S(2)}) async-start(), calls=%async_computation.4 | async-start | bytes 5242880 | tf_op jit(solution)/shard_map/all_gather | solution.py:69
  531.8 8.6 copy-start.49
  540.5 69.4 %collective-permute-start.6 = (bf16[768,2048]{1,0:T(8,128)(2,1)S(1)}, bf16[768,2048]{1,0:T(8,128)(2,1)}, u32[]{:S(2)}, u32[]{:S(2)}) collective-permute-start(bf16[768,2048]{1,0:T(8,128)(2,1)S(1)} %get-tuple-element.40), channel_id=1, source_target_pairs={{0,4},{4,0},{1,5},{5,1},{2,6},{6,2},{3,7},{7,3},{8,12},{12,8},{9,1... | collective-permute-start | bytes 9437192 | tf_op jit(solution)/shard_map/ppermute | solution.py:16
  584.0 181.6 %all-gather.17.cloned.1.call-start = ((), (), s32[]{:S(2)}) async-start(), calls=%async_computation.5 | async-start | bytes 5242880 | tf_op jit(solution)/shard_map/all_gather | solution.py:69
  612.2 4.6 copy-start.3
  616.8 71.0 %collective-permute-start.7 = (bf16[768,4096]{1,0:T(8,128)(2,1)}, bf16[768,4096]{1,0:T(8,128)(2,1)}, u32[]{:S(2)}, u32[]{:S(2)}) collective-permute-start(bf16[768,4096]{1,0:T(8,128)(2,1)} %pad_maximum_fusion.3), channel_id=1, source_target_pairs={{0,8},{8,0},{1,9},{9,1},{2,10},{10,2},{3,11},{11,3},{4,12},{12,4},... | collective-permute-start | bytes 18874376 | tf_op jit(solution)/shard_map/ppermute | solution.py:16
  616.8 70.8 %collective-permute-start.9 = (bf16[2048,768]{1,0:T(8,128)(2,1)}, bf16[2048,768]{1,0:T(8,128)(2,1)}, u32[]{:S(2)}, u32[]{:S(2)}) collective-permute-start(bf16[2048,768]{1,0:T(8,128)(2,1)} %pad_maximum_fusion.6), channel_id=1, source_target_pairs={{0,16},{16,0},{1,17},{17,1},{2,18},{18,2},{3,19},{19,3},{4,20},{20... | collective-permute-start | bytes 9437192 | tf_op jit(solution)/shard_map/ppermute | solution.py:16
  665.1 22.6 %copy-start.29 = (bf16[2048,256]{1,0:T(8,128)(2,1)}, bf16[2048,256]{1,0:T(8,128)(2,1)S(1)}, u32[]{:S(2)}) copy-start(bf16[2048,256]{1,0:T(8,128)(2,1)S(1)} %get-tuple-element.114) | copy-start | bytes 3145732
  702.1 6.2 copy-start
  714.8 8.0 copy-start.14
  714.8 8.0 copy-start.16
  714.8 8.0 copy-start.18
  721.3 71.3 %collective-permute-start.10 = (bf16[2048,768]{1,0:T(8,128)(2,1)}, bf16[2048,768]{1,0:T(8,128)(2,1)}, u32[]{:S(2)}, u32[]{:S(2)}) collective-permute-start(bf16[2048,768]{1,0:T(8,128)(2,1)} %pad_maximum_fusion.7), channel_id=1, source_target_pairs={{0,16},{16,0},{1,17},{17,1},{2,18},{18,2},{3,19},{19,3},{4,20},{20... | collective-permute-start | bytes 9437192 | tf_op jit(solution)/shard_map/ppermute | solution.py:16
  765.6 4.1 copy-start.20
  765.6 4.1 copy-start.22
  765.6 4.1 copy-start.24
  765.6 4.1 copy-start.46
  765.6 4.1 copy-start.47
  765.6 4.1 copy-start.48
  767.9 6.5 slice-start
  768.2 90.6 %collective-permute-start.11 = (bf16[2048,768]{1,0:T(8,128)(2,1)S(1)}, bf16[2048,768]{1,0:T(8,128)(2,1)}, u32[]{:S(2)}, u32[]{:S(2)}) collective-permute-start(bf16[2048,768]{1,0:T(8,128)(2,1)S(1)} %pad_maximum_fusion.8), channel_id=1, source_target_pairs={{0,16},{16,0},{1,17},{17,1},{2,18},{18,2},{3,19},{19,3},{4,20},{20... | collective-permute-start | bytes 9437192 | tf_op jit(solution)/shard_map/ppermute | solution.py:16
  769.7 4.6 slice-start.1
  774.4 10.2 %copy-start.26 = (bf16[2048,256]{1,0:T(8,128)(2,1)S(1)}, bf16[2048,256]{1,0:T(8,128)(2,1)}, u32[]{:S(2)}) copy-start(bf16[2048,256]{1,0:T(8,128)(2,1)} %copy-done.25) | copy-start | bytes 3145732
  774.4 10.2 %copy-start.28 = (bf16[2048,256]{1,0:T(8,128)(2,1)S(1)}, bf16[2048,256]{1,0:T(8,128)(2,1)}, u32[]{:S(2)}) copy-start(bf16[2048,256]{1,0:T(8,128)(2,1)} %copy-done.27) | copy-start | bytes 3145732
  774.4 10.1 %copy-start.30 = (bf16[2048,256]{1,0:T(8,128)(2,1)S(1)}, bf16[2048,256]{1,0:T(8,128)(2,1)}, u32[]{:S(2)}) copy-start(bf16[2048,256]{1,0:T(8,128)(2,1)} %copy-done.29) | copy-start | bytes 3145732
  774.4 10.1 %copy-start.43 = (bf16[768,256]{1,0:T(8,128)(2,1)S(1)}, bf16[768,256]{1,0:T(8,128)(2,1)}, u32[]{:S(2)}) copy-start(bf16[768,256]{1,0:T(8,128)(2,1)} %get-tuple-element.58) | copy-start | bytes 1179652
  774.4 10.1 %copy-start.44 = (bf16[768,256]{1,0:T(8,128)(2,1)S(1)}, bf16[768,256]{1,0:T(8,128)(2,1)}, u32[]{:S(2)}) copy-start(bf16[768,256]{1,0:T(8,128)(2,1)} %get-tuple-element.59) | copy-start | bytes 1179652
  774.4 10.1 %copy-start.45 = (bf16[768,256]{1,0:T(8,128)(2,1)S(1)}, bf16[768,256]{1,0:T(8,128)(2,1)}, u32[]{:S(2)}) copy-start(bf16[768,256]{1,0:T(8,128)(2,1)} %get-tuple-element.60) | copy-start | bytes 1179652
  784.5 8.1 copy-start.40
  784.6 8.1 copy-start.41
  784.6 8.1 copy-start.42
  792.7 6.6 copy-start.37
  792.7 6.6 copy-start.38
  792.7 6.6 copy-start.39
  894.0 9.2 copy-start.1
  908.0 26.9 %collective-permute-start.12 = (bf16[768,2048]{1,0:T(8,128)(2,1)}, bf16[768,2048]{1,0:T(8,128)(2,1)}, u32[]{:S(2)}, u32[]{:S(2)}) collective-permute-start(bf16[768,2048]{1,0:T(8,128)(2,1)} %get-tuple-element.33), channel_id=1, source_target_pairs={{0,8},{8,0},{1,9},{9,1},{2,10},{10,2},{3,11},{11,3},{4,12},{12,4},... | collective-permute-start | bytes 9437192 | tf_op jit(solution)/shard_map/ppermute | solution.py:16
  (11 other events, 28.8 us)
Sparse Core Ops, SparseCore 0:
  46.0 152.2 all-gather.6
  205.8 147.8 all-gather.8
  363.1 77.8 all-gather.10
  500.3 78.7 all-gather.12
  584.2 78.7 all-gather.14
  687.8 77.7 all-gather.16

commit v3 on v2

--- a/solution.py
+++ b/solution.py
@@ -50,7 +50,21 @@
         given = lax.dynamic_slice_in_dim(value, (1 - core) * half, half, axis)
         return per_section(mine, shifted(given, "section"))
 
-    weight_of = over_cores(weights[0], 0)
+    units = max(1, part // 128)
+    step_units = max(1, units // 4)
+    unit = part // units
+    widths_of = {}
+    for section in (1, 0):
+        sizes = [step_units] * (units // step_units)
+        if sum(sizes) < units:
+            sizes.append(units - sum(sizes))
+        widths_of[section] = [size * unit for size in sizes]
+    mine = lax.dynamic_slice_in_dim(weights[0], core * half, half, 0)
+    given = lax.dynamic_slice_in_dim(weights[0], (1 - core) * half, half, 0)
+    lead = widths_of[1][0]
+    lead_given = shifted(columns(given, group * part, lead), "section")
+    first_pieces = per_section(columns(mine, group * part, lead), lead_given)
+    weight_of = per_section(mine, shifted(after(given, lead_given), "section"))
     hidden_of = over_cores(hidden[0].reshape(tokens, features), 1)
     gain_of = over_cores(norm_gains[0], 0)
     steer_vec = own_columns(steering).astype(f32)
@@ -59,35 +73,35 @@
 
     earlier, sent = [], []
     pieces = {}
-    for section, count in ((1, 2), (0, 4)):
-        count = max(1, min(count, part // 128))
-        width = part // count
+    for section in (1, 0):
         held = []
-        for chunk in range(count):
-            own = columns(weight_of[section], group * part + chunk * width, width)
-            own = after(own, tuple(earlier))
+        start = 0
+        for width in widths_of[section]:
+            own = first_pieces[section] if start == 0 else columns(weight_of[section], group * part + start, width)
+            if earlier:
+                own = after(own, tuple(earlier))
             gathered = lax.all_gather(own, "col", axis=1, tiled=True)
             others = jnp.concatenate(
                 [columns(gathered, ((col_index + step) % cols) * width, width) for step in range(1, cols)], 1
             )
-            held.append((others, shifted(others, "groups")))
-            earlier = [others] + [held_before[1] for held_before in sent[-1:]]
-            sent.append(held[-1])
-        pieces[section] = (width, held)
+            held.append((start, width, (others, shifted(others, "groups"))))
+            earlier = [others] + sent[-1:]
+            sent.append(held[-1][2][1])
+            start += width
+        pieces[section] = held
 
     def projected(full, section):
-        width, held = pieces[section]
-
         def times(left, right):
             return lax.dot_general(left, right, (((1,), (1,)), ((), ())), preferred_element_type=f32)
 
         total = times(columns(full, col_index * depth, depth), weight_of[section])
-        for chunk, sides in enumerate(held):
+        held = pieces[section]
+        for start, width, sides in held:
+            total = lax.optimization_barrier(total)
             for side, block in enumerate(sides):
-                owner = (group + side) % groups
-                start = owner * part + chunk * width
+                offset = ((group + side) % groups) * part + start
                 left = jnp.concatenate(
-                    [columns(full, ((col_index + step) % cols) * depth + start, width) for step in range(1, cols)], 1
+                    [columns(full, ((col_index + step) % cols) * depth + offset, width) for step in range(1, cols)], 1
                 )
                 total = total + times(left, block)
         return total

time: 954 us -> 921 us (0.965)
  waiting for transfers between devices: 602 us -> 561 us
  other arithmetic: 84.9 us -> 98.9 us
  matrix products: 132 us -> 120 us
    all_gather x6 -> x8, waiting for transfers between devices: 432 us -> 404 us  [local(): gathered = lax.all_gather(own, 'col', axis=1, tiled=True)]
    ppermute x13 -> x16, waiting for transfers between devices: 170 us -> 156 us  [shifted(): lax.ppermute(value, axis, [(source, (source + steps) % count) for source...]
    dot_general x14 -> x18, matrix products: 132 us -> 120 us  [times(): lax.dot_general(left, right, (((1,), (1,)), ((), ())), preferred_element_...]
    dynamic_slice x10 -> x13, local copies, waits for them, and re-layouts: 25.7 us -> 28.4 us  [columns(): return lax.dynamic_slice_in_dim(value, start, width, value.ndim - 1)]
  transfers between devices with their start and end apart: 19 -> 24, of which waited for: 12 -> 15; matrix products, arithmetic and copies ran while one was open for 20% -> 24% of each run, Pallas kernels for 0% -> 0%
where the time goes in v3:
time: 921 us; the launch traced here: 915 us
  waiting for transfers between devices  561 us (61%)
  matrix products  120 us (13%)
  other arithmetic  98.9 us (11%)
  local copies, waits for them, and re-layouts  56.9 us (6%)
  blocking collectives  48.9 us (5%)
  between operations  15.7 us (2%)
  starting transfers between devices  14.6 us (2%)
    all_gather x8, waiting for transfers between devices, local(): gathered = lax.all_gather(own, 'col', axis=1, tiled=True)  404 us
    ppermute x16, waiting for transfers between devices, shifted(): lax.ppermute(value, axis, [(source, (source + steps) % count) for source...  156 us
    dot_general x18, matrix products, times(): lax.dot_general(left, right, (((1,), (1,)), ((), ())), preferred_element_...  120 us
    dynamic_slice x13, local copies, waits for them, and re-layouts, columns(): return lax.dynamic_slice_in_dim(value, start, width, value.ndim - 1)  28.4 us
    psum x1, blocking collectives, local(): steer_total = lax.psum(slots, ('section', 'col'))  27 us
    psum x2, blocking collectives, local(): sums = lax.psum(tuple(local_sums), ('row', 'section'))  21.9 us
  transfers between devices with their start and end apart: 24, of which 15 were waited for; matrix products, arithmetic and copies ran while one was open for 24% of the time, Pallas kernels for 0%

profile of v3, /device:TPU:0, one launch (start us, length us, event | category | flops | bytes accessed | tf_op | source)
XLA Modules:
  0.0 915.4 jit_solution(15093724185360107491)
XLA Ops:
  9.8 8.4 dynamic-slice_bitcast_fusion
  18.3 3.7 bitcast_select_fusion.2
  22.0 83.3 %all-gather.9.cloned.1.call-done = bf16[2048,1024]{1,0:T(8,128)(2,1)} async-done(((bf16[2048,256]{1,0:T(8,128)(2,1)}), bf16[2048,1024]{1,0:T(8,128)(2,1)}) %all-gather.9.cloned.1.call-update) | async-done | bytes 4194320 | tf_op jit(solution)/shard_map/all_gather | solution.py:83
  105.4 2.1 constant_dynamic-slice_fusion.53
  109.2 10.9 %bitcast_select_fusion = (bf16[2048,2048]{1,0:T(8,128)(2,1)}, bf16[2048,2048]{1,0:T(8,128)(2,1)S(1)}) fusion(bf16[2048,2048]{1,0:T(8,128)(2,1)} %collective-permute-done.4, pred[]{:T(512)S(6)} %eq.150, bf16[1,4096,2048]{2,1,0:T(8,128)(2,1)} %param.8, s32[]{:T(128)S(6)} %select_n.500, pred[]{:T(512)S(6)} %eq.157), kind=kLoop, calls=%fused_computation.65 | loop fusion | flops 8388608 | bytes 33554440 | tf_op jit(solution)/shard_map/jit(_where)/select_n | solution.py:46
  120.2 3.3 copy-done.4
  126.9 77.3 %all-gather.11.cloned.1.call-done = bf16[2048,1024]{1,0:T(8,128)(2,1)} async-done(((bf16[2048,256]{1,0:T(8,128)(2,1)}), bf16[2048,1024]{1,0:T(8,128)(2,1)}) %all-gather.11.cloned.1.call-update) | async-done | bytes 4194320 | tf_op jit(solution)/shard_map/all_gather | solution.py:83
  204.2 2.1 constant_dynamic-slice_fusion.49
  212.2 75.8 %all-gather.13.cloned.1.call-done = bf16[2048,1024]{1,0:T(8,128)(2,1)} async-done(((bf16[2048,256]{1,0:T(8,128)(2,1)}), bf16[2048,1024]{1,0:T(8,128)(2,1)}) %all-gather.13.cloned.1.call-update) | async-done | bytes 4194320 | tf_op jit(solution)/shard_map/all_gather | solution.py:83
  288.1 2.1 constant_dynamic-slice_fusion.45
  293.4 3.9 constant_dynamic-slice_fusion.56
  300.6 47.6 %collective-permute-done.2 = bf16[768,4096]{1,0:T(8,128)(2,1)} collective-permute-done((bf16[768,4096]{1,0:T(8,128)(2,1)}, bf16[768,4096]{1,0:T(8,128)(2,1)}, u32[]{:S(2)}, u32[]{:S(2)}) %collective-permute-start.2) | collective-permute-done | bytes 6291488 | tf_op jit(solution)/shard_map/ppermute | solution.py:16
  348.3 5.2 broadcast_select_fusion.2
  353.5 2.9 fusion.148
  356.4 3.0 fusion.151
  359.4 2.5 fusion.152
  361.9 10.0 %all-gather.15.cloned.1.call-done = bf16[2048,1024]{1,0:T(8,128)(2,1)} async-done(((bf16[2048,256]{1,0:T(8,128)(2,1)}), bf16[2048,1024]{1,0:T(8,128)(2,1)}) %all-gather.15.cloned.1.call-update) | async-done | bytes 4194320 | tf_op jit(solution)/shard_map/all_gather | solution.py:83
  376.9 3.8 fusion.129
  380.8 4.9 fusion.35
  385.7 11.3 %fusion.31 = f32[768,2048]{1,0:T(8,128)} fusion(bf16[2048,2048]{1,0:T(8,128)(2,1)} %copy-done.4, s32[]{:T(128)S(6)} %select_n.510, bf16[768,4096]{1,0:T(8,128)(2,1)S(1)} %bitcast.31, bf16[768,4096]{1,0:T(8,128)(2,1)S(1)} %bitcast.29), kind=kOutput, calls=%fused_computation.111 | convolution fusion | flops 6448742400 | bytes 27262980 | tf_op jit(solution)/shard_map/dot_general | solution.py:95
  397.0 3.8 constant_dynamic-slice_fusion.6
  401.9 6.2 add_add_fusion.5
  409.7 3.8 fusion.46
  413.6 4.8 add_add_fusion.4
  418.4 3.8 fusion.57
  422.3 6.5 add_add_fusion.3
  428.8 26.9 %all-gather.17.cloned.1.call-done = bf16[2048,1024]{1,0:T(8,128)(2,1)} async-done(((bf16[2048,256]{1,0:T(8,128)(2,1)}), bf16[2048,1024]{1,0:T(8,128)(2,1)}) %all-gather.17.cloned.1.call-update) | async-done | bytes 4194320 | tf_op jit(solution)/shard_map/all_gather | solution.py:83
  458.8 2.2 pad_maximum_fusion.7
  461.0 17.5 %collective-permute-done.8 = bf16[2048,768]{1,0:T(8,128)(2,1)} collective-permute-done((bf16[2048,768]{1,0:T(8,128)(2,1)}, bf16[2048,768]{1,0:T(8,128)(2,1)}, u32[]{:S(2)}, u32[]{:S(2)}) %collective-permute-start.8) | collective-permute-done | bytes 3145760 | tf_op jit(solution)/shard_map/ppermute | solution.py:16
  478.6 7.2 fusion.68
  485.9 12.3 %fusion.23 = (f32[768]{0:T(1024)S(1)}, f32[768]{0:T(1024)S(1)}, f32[768]{0:T(1024)S(1)}, f32[768]{0:T(1024)S(1)}, bf16[768,2048]{1,0:T(8,128)(2,1)}, /*index=5*/f32[768,2048]{1,0:T(8,128)}) fusion(f32[2048]{0:T(1024)S(1)} %dynamic-slice_convert_fusion, bf16[768,4096]{1,0:T(8,128)(2,1)S(1)} %bitcast.38, s32[]{:T(128)S(6)} %select_n.500, ...), kind=kOutput, calls=%fused_computation.87 | convolution fusion | flops 2444620800 | bytes 35812100 | tf_op jit(solution)/shard_map/dot_general | solution.py:95
  498.2 10.9 %all-reduce.1 = (f32[768]{0:T(1024)S(1)}, f32[768]{0:T(1024)S(1)}, f32[768]{0:T(1024)S(1)}, f32[768]{0:T(1024)S(1)}) all-reduce(f32[768]{0:T(1024)S(1)} %get-tuple-element.25, f32[768]{0:T(1024)S(1)} %get-tuple-element.22, f32[768]{0:T(1024)S(1)} %get-tuple-element.23, ...), channel_id=1, replica_groups=mesh['groups'=2,'section'=2,'row'=2,'col'=4] {'row','section'}, use_global_device_ids=true, to_apply=%region_5.6 | all-reduce | flops 3072 | bytes 24576 | tf_op jit(solution)/shard_map/psum | solution.py:128
  512.2 8.7 fusion.29
  522.4 35.1 %all-gather.19.cloned.1.call-done = bf16[2048,1024]{1,0:T(8,128)(2,1)} async-done(((bf16[2048,256]{1,0:T(8,128)(2,1)}), bf16[2048,1024]{1,0:T(8,128)(2,1)}) %all-gather.19.cloned.1.call-update) | async-done | bytes 4194320 | tf_op jit(solution)/shard_map/all_gather | solution.py:83
  557.5 2.1 constant_dynamic-slice_fusion.25
  562.3 18.0 %collective-permute-done.11 = bf16[2048,768]{1,0:T(8,128)(2,1)} collective-permute-done((bf16[2048,768]{1,0:T(8,128)(2,1)}, bf16[2048,768]{1,0:T(8,128)(2,1)}, u32[]{:S(2)}, u32[]{:S(2)}) %collective-permute-start.11) | collective-permute-done | bytes 3145760 | tf_op jit(solution)/shard_map/ppermute | solution.py:16
  580.5 9.6 %collective-permute-done.9 = bf16[768,2048]{1,0:T(8,128)(2,1)} collective-permute-done((bf16[768,2048]{1,0:T(8,128)(2,1)S(1)}, bf16[768,2048]{1,0:T(8,128)(2,1)}, u32[]{:S(2)}, u32[]{:S(2)}) %collective-permute-start.9) | collective-permute-done | bytes 3145760 | tf_op jit(solution)/shard_map/ppermute | solution.py:16
  590.1 2.4 broadcast_select_fusion.5
  592.4 3.8 pad_maximum_fusion.1
  598.2 60.7 %all-gather.21.cloned.1.call-done = bf16[2048,1024]{1,0:T(8,128)(2,1)} async-done(((bf16[2048,256]{1,0:T(8,128)(2,1)}), bf16[2048,1024]{1,0:T(8,128)(2,1)}) %all-gather.21.cloned.1.call-update) | async-done | bytes 4194320 | tf_op jit(solution)/shard_map/all_gather | solution.py:83
  664.1 3.9 collective-permute-done.12
  668.0 6.7 broadcast_select_fusion.1
  675.3 3.3 fusion.186
  678.7 4.6 pad_maximum_fusion
  683.3 9.3 %fusion.33 = f32[768,2048]{1,0:T(8,128)S(1)} fusion(bf16[2048,2048]{1,0:T(8,128)(2,1)} %get-tuple-element.53, bf16[768,8192]{1,0:T(8,128)(2,1)S(1)} %pad_maximum_fusion, s32[]{:T(128)S(6)} %select_n.510), kind=kOutput, calls=%fused_computation.120 | convolution fusion | flops 6442450944 | bytes 17825796 | tf_op jit(solution)/shard_map/dot_general | solution.py:95
  693.7 4.6 fusion.82
  698.6 9.4 %add_add_fusion.2 = f32[768,2048]{1,0:T(8,128)} fusion(f32[768,2048]{1,0:T(8,128)S(1)} %fusion.33, f32[768,2048]{1,0:T(8,128)} %fusion.82, bf16[2048,768]{1,0:T(8,128)(2,1)} %collective-permute-done.11, bf16[768,256]{1,0:T(8,128)(2,1)S(1)} %get-tuple-element.76, bf16[768,256]{1,0:T(8,128)(2,1)} %get-tuple-element.77, ...), kind=kOutput, calls=%fused_computation.101 | convolution fusion | flops 2422603776 | bytes 23199744 | tf_op jit(solution)/shard_map/dot_general | solution.py:95
  708.0 2.8 constant_dynamic-slice_fusion.2
  710.8 34.9 %all-gather.23.cloned.1.call-done = bf16[2048,1024]{1,0:T(8,128)(2,1)} async-done(((bf16[2048,256]{1,0:T(8,128)(2,1)}), bf16[2048,1024]{1,0:T(8,128)(2,1)}) %all-gather.23.cloned.1.call-update) | async-done | bytes 4194320 | tf_op jit(solution)/shard_map/all_gather | solution.py:83
  745.7 2.3 constant_dynamic-slice_fusion.5
  751.6 2.6 fusion.93
  754.3 4.9 add_add_fusion.1
  759.3 4.6 fusion.104
  763.9 5.8 collective-permute-done.13
  769.6 4.8 add_add_fusion
  774.5 7.3 fusion.115
  781.8 53.9 %collective-permute-done.14 = bf16[2048,768]{1,0:T(8,128)(2,1)} collective-permute-done((bf16[2048,768]{1,0:T(8,128)(2,1)}, bf16[2048,768]{1,0:T(8,128)(2,1)}, u32[]{:S(2)}, u32[]{:S(2)}) %collective-permute-start.14) | collective-permute-done | bytes 3145760 | tf_op jit(solution)/shard_map/ppermute | solution.py:16
  835.8 11.5 %fusion.15 = (f32[768]{0:T(1024)}, f32[768]{0:T(1024)}, f32[768]{0:T(1024)}, f32[768]{0:T(1024)}, bf16[768,2048]{1,0:T(8,128)(2,1)}, /*index=5*/f32[768,2048]{1,0:T(8,128)}) fusion(bf16[768,2048]{1,0:T(8,128)(2,1)S(1)} %get-tuple-element.46, f32[2048]{0:T(1024)S(1)} %dynamic-slice_convert_fusion, pred[768]{0:T(1024)(128)(4,1)S(1)} %copy-done.68, ...), kind=kOutput, calls=%fused_computation.79 | convolution fusion | flops 2444620800 | bytes 35812100 | tf_op jit(solution)/shard_map/dot_general | solution.py:95
  847.3 11.0 %all-reduce = (f32[768]{0:T(1024)S(1)}, f32[768]{0:T(1024)S(1)}, f32[768]{0:T(1024)S(1)}, f32[768]{0:T(1024)S(1)}) all-reduce(f32[768]{0:T(1024)} %get-tuple-element.24, f32[768]{0:T(1024)} %get-tuple-element.19, f32[768]{0:T(1024)} %get-tuple-element.20, ...), channel_id=1, replica_groups=mesh['groups'=2,'section'=2,'row'=2,'col'=4] {'row','section'}, use_global_device_ids=true, to_apply=%region_1.2 | all-reduce | flops 3072 | bytes 24576 | tf_op jit(solution)/shard_map/psum | solution.py:128
  859.6 9.2 %select_reduce_fusion = (f32[2048]{0:T(1024)S(1)}, f32[2048]{0:T(1024)S(1)}, f32[768,2048]{1,0:T(8,128)S(1)}) fusion(bf16[768,2048]{1,0:T(8,128)(2,1)} %get-tuple-element.45, f32[768]{0:T(1024)S(1)} %get-tuple-element.41, f32[768]{0:T(1024)S(1)} %get-tuple-element.44, f32[2048]{0:T(1024)S(1)} %dynamic-slice_convert_fusion, pred[768]{0:T(1024)(128)(4,1)} %eq.153, ...), kind=kLoop, calls=%fused_computation.96 | loop fusion | flops 31453184 | bytes 28356096 | tf_op jit(solution)/shard_map/reduce_sum | solution.py:161
  868.9 4.7 broadcast_select_fusion.9
  873.7 27.0 %psum.71 = f32[4096]{0:T(1024)S(1)} all-reduce(f32[4096]{0:T(1024)S(1)} %bitcast.43), channel_id=1, replica_groups=mesh['groups'=2,'section'=2,'row'=2,'col'=4] {'section','col'}, use_global_device_ids=true, to_apply=%region_18.19 | all-reduce | flops 4096 | bytes 32768 | tf_op jit(solution)/shard_map/psum | solution.py:171
  901.4 3.4 broadcast_select_fusion.8
  904.7 3.5 pad_maximum_fusion.2
  (242 shorter events, 53.0 us)
Async XLA Ops:
  7.2 98.2 %all-gather.9.cloned.1.call-start = ((), (), s32[]{:S(2)}) async-start(), calls=%async_computation | async-start | bytes 5242880 | tf_op jit(solution)/shard_map/all_gather | solution.py:83
  9.3 8.9 collective-permute-start.3
  18.2 91.0 %collective-permute-start.4 = (bf16[2048,2048]{1,0:T(8,128)(2,1)}, bf16[2048,2048]{1,0:T(8,128)(2,1)}, u32[]{:S(2)}, u32[]{:S(2)}) collective-permute-start(bf16[2048,2048]{1,0:T(8,128)(2,1)} %dynamic-slice_bitcast_fusion), channel_id=1, source_target_pairs={{0,8},{8,0},{1,9},{9,1},{2,10},{10,2},{3,11},{11,3},{4,12},{12,4},... | collective-permute-start | bytes 25165832 | tf_op jit(solution)/shard_map/ppermute | solution.py:16
  21.9 182.3 %all-gather.11.cloned.1.call-start = ((), (), s32[]{:S(2)}) async-start(), calls=%async_computation.1 | async-start | bytes 5242880 | tf_op jit(solution)/shard_map/all_gather | solution.py:83
  125.3 162.8 %all-gather.13.cloned.1.call-start = ((), (), s32[]{:S(2)}) async-start(), calls=%async_computation.2 | async-start | bytes 5242880 | tf_op jit(solution)/shard_map/all_gather | solution.py:83
  125.3 83.8 %collective-permute-start.5 = (bf16[2048,768]{1,0:T(8,128)(2,1)}, bf16[2048,768]{1,0:T(8,128)(2,1)}, u32[]{:S(2)}, u32[]{:S(2)}) collective-permute-start(bf16[2048,768]{1,0:T(8,128)(2,1)} %pad_maximum_fusion.3), channel_id=1, source_target_pairs={{0,16},{16,0},{1,17},{17,1},{2,18},{18,2},{3,19},{19,3},{4,20},{20... | collective-permute-start | bytes 9437192 | tf_op jit(solution)/shard_map/ppermute | solution.py:16
  209.2 162.7 %all-gather.15.cloned.1.call-start = ((), (), s32[]{:S(2)}) async-start(), calls=%async_computation.3 | async-start | bytes 5242880 | tf_op jit(solution)/shard_map/all_gather | solution.py:83
  209.2 83.8 %collective-permute-start.6 = (bf16[2048,768]{1,0:T(8,128)(2,1)}, bf16[2048,768]{1,0:T(8,128)(2,1)}, u32[]{:S(2)}, u32[]{:S(2)}) collective-permute-start(bf16[2048,768]{1,0:T(8,128)(2,1)} %pad_maximum_fusion.4), channel_id=1, source_target_pairs={{0,16},{16,0},{1,17},{17,1},{2,18},{18,2},{3,19},{19,3},{4,20},{20... | collective-permute-start | bytes 9437192 | tf_op jit(solution)/shard_map/ppermute | solution.py:16
  210.8 82.5 %copy-start.70 = (bf16[1,4096]{1,0:T(2,128)(2,1)S(1)}, bf16[1,4096]{1,0:T(2,128)(2,1)}, u32[]{:S(2)}) copy-start(bf16[1,4096]{1,0:T(2,128)(2,1)} %param.9) | copy-start | bytes 24580
  210.8 137.5 %collective-permute-start.2 = (bf16[768,4096]{1,0:T(8,128)(2,1)}, bf16[768,4096]{1,0:T(8,128)(2,1)}, u32[]{:S(2)}, u32[]{:S(2)}) collective-permute-start(bf16[768,4096]{1,0:T(8,128)(2,1)} %bitcast.34), channel_id=1, source_target_pairs={{0,4},{4,0},{1,5},{5,1},{2,6},{6,2},{3,7},{7,3},{8,12},{12,8},{9,1... | collective-permute-start | bytes 18874376 | tf_op jit(solution)/shard_map/ppermute | solution.py:16
  291.2 8.1 copy-start.75
  291.2 8.1 copy-start.74
  293.0 162.7 %all-gather.17.cloned.1.call-start = ((), (), s32[]{:S(2)}) async-start(), calls=%async_computation.4 | async-start | bytes 5242880 | tf_op jit(solution)/shard_map/all_gather | solution.py:83
  293.3 6.7 collective-permute-start.1
  297.3 188.6 %collective-permute-start = (bf16[768,2048]{1,0:T(8,128)(2,1)}, bf16[768,2048]{1,0:T(8,128)(2,1)}, u32[]{:S(2)}, u32[]{:S(2)}) collective-permute-start(bf16[768,2048]{1,0:T(8,128)(2,1)} %constant_dynamic-slice_fusion.56), channel_id=1, source_target_pairs={{0,8},{8,0},{1,9},{9,1},{2,10},{10,2},{3,11},{11,3},{4,12},{12,4},... | collective-permute-start | bytes 9437192 | tf_op jit(solution)/shard_map/ppermute | solution.py:16
  297.8 78.9 %collective-permute-start.7 = (bf16[2048,768]{1,0:T(8,128)(2,1)}, bf16[2048,768]{1,0:T(8,128)(2,1)}, u32[]{:S(2)}, u32[]{:S(2)}) collective-permute-start(bf16[2048,768]{1,0:T(8,128)(2,1)} %pad_maximum_fusion.5), channel_id=1, source_target_pairs={{0,16},{16,0},{1,17},{17,1},{2,18},{18,2},{3,19},{19,3},{4,20},{20... | collective-permute-start | bytes 9437192 | tf_op jit(solution)/shard_map/ppermute | solution.py:16
  299.9 186.0 %copy-start.67 = (pred[768]{0:T(1024)(128)(4,1)}, pred[768]{0:T(1024)(128)(4,1)S(1)}, u32[]{:S(2)}) copy-start(pred[768]{0:T(1024)(128)(4,1)S(1)} %eq.156) | copy-start | bytes 2308
  353.5 5.9 copy-start
  353.5 5.9 copy-start.1
  376.8 180.8 %all-gather.19.cloned.1.call-start = ((), (), s32[]{:S(2)}) async-start(), calls=%async_computation.5 | async-start | bytes 5242880 | tf_op jit(solution)/shard_map/all_gather | solution.py:83
  376.9 8.8 slice-start
  376.9 8.8 slice-start.2
  385.7 15.1 %copy-start.48 = (bf16[768,256]{1,0:T(8,128)(2,1)S(1)}, bf16[768,256]{1,0:T(8,128)(2,1)}, u32[]{:S(2)}) copy-start(bf16[768,256]{1,0:T(8,128)(2,1)} %get-tuple-element.87) | copy-start | bytes 1179652
  385.7 15.1 %copy-start.49 = (bf16[768,256]{1,0:T(8,128)(2,1)S(1)}, bf16[768,256]{1,0:T(8,128)(2,1)}, u32[]{:S(2)}) copy-start(bf16[768,256]{1,0:T(8,128)(2,1)} %get-tuple-element.88) | copy-start | bytes 1179652
  385.7 15.0 %copy-start.50 = (bf16[768,256]{1,0:T(8,128)(2,1)S(1)}, bf16[768,256]{1,0:T(8,128)(2,1)}, u32[]{:S(2)}) copy-start(bf16[768,256]{1,0:T(8,128)(2,1)} %get-tuple-element.90) | copy-start | bytes 1179652
  401.9 7.7 copy-start.8
  401.9 7.7 copy-start.10
  401.9 7.7 copy-start.12
  401.9 7.7 copy-start.62
  408.1 70.4 %collective-permute-start.8 = (bf16[2048,768]{1,0:T(8,128)(2,1)}, bf16[2048,768]{1,0:T(8,128)(2,1)}, u32[]{:S(2)}, u32[]{:S(2)}) collective-permute-start(bf16[2048,768]{1,0:T(8,128)(2,1)} %pad_maximum_fusion.6), channel_id=1, source_target_pairs={{0,16},{16,0},{1,17},{17,1},{2,18},{18,2},{3,19},{19,3},{4,20},{20... | collective-permute-start | bytes 9437192 | tf_op jit(solution)/shard_map/ppermute | solution.py:16
  428.8 49.7 %copy-start.36 = (bf16[2048,256]{1,0:T(8,128)(2,1)S(1)}, bf16[2048,256]{1,0:T(8,128)(2,1)}, u32[]{:S(2)}) copy-start(bf16[2048,256]{1,0:T(8,128)(2,1)} %copy-done.35) | copy-start | bytes 3145732
  428.8 49.8 %copy-start.60 = (bf16[768,256]{1,0:T(8,128)(2,1)S(1)}, bf16[768,256]{1,0:T(8,128)(2,1)}, u32[]{:S(2)}) copy-start(bf16[768,256]{1,0:T(8,128)(2,1)} %get-tuple-element.101) | copy-start | bytes 1179652
  457.8 20.7 %copy-start.23 = (bf16[2048,256]{1,0:T(8,128)(2,1)}, bf16[2048,256]{1,0:T(8,128)(2,1)S(1)}, u32[]{:S(2)}) copy-start(bf16[2048,256]{1,0:T(8,128)(2,1)S(1)} %get-tuple-element.134) | copy-start | bytes 3145732
  458.8 27.1 %slice-start.6 = ((s8[6291456]{0:T(1024)(128)(4,1)}), s8[2097152]{0:T(1024)(128)(4,1)S(1)}, s32[]{:S(2)}) async-start(s8[6291456]{0:T(1024)(128)(4,1)} %bitcast.36), calls=%async_computation.14 | async-start | bytes 4194304
  478.5 180.5 %all-gather.21.cloned.1.call-start = ((), (), s32[]{:S(2)}) async-start(), calls=%async_computation.6 | async-start | bytes 5242880 | tf_op jit(solution)/shard_map/all_gather | solution.py:83
  478.6 7.3 slice-start.7
  478.6 7.3 copy-start.58
  478.6 7.3 copy-start.59
  478.6 7.3 copy-start.61
  478.6 7.3 copy-start.72
  510.6 69.8 %collective-permute-start.11 = (bf16[2048,768]{1,0:T(8,128)(2,1)}, bf16[2048,768]{1,0:T(8,128)(2,1)}, u32[]{:S(2)}, u32[]{:S(2)}) collective-permute-start(bf16[2048,768]{1,0:T(8,128)(2,1)} %pad_maximum_fusion.7), channel_id=1, source_target_pairs={{0,16},{16,0},{1,17},{17,1},{2,18},{18,2},{3,19},{19,3},{4,20},{20... | collective-permute-start | bytes 9437192 | tf_op jit(solution)/shard_map/ppermute | solution.py:16
  520.9 69.1 %collective-permute-start.9 = (bf16[768,2048]{1,0:T(8,128)(2,1)S(1)}, bf16[768,2048]{1,0:T(8,128)(2,1)}, u32[]{:S(2)}, u32[]{:S(2)}) collective-permute-start(bf16[768,2048]{1,0:T(8,128)(2,1)S(1)} %get-tuple-element.46), channel_id=1, source_target_pairs={{0,4},{4,0},{1,5},{5,1},{2,6},{6,2},{3,7},{7,3},{8,12},{12,8},{9,1... | collective-permute-start | bytes 9437192 | tf_op jit(solution)/shard_map/ppermute | solution.py:16
  559.7 20.7 %copy-start.29 = (bf16[2048,256]{1,0:T(8,128)(2,1)}, bf16[2048,256]{1,0:T(8,128)(2,1)S(1)}, u32[]{:S(2)}) copy-start(bf16[2048,256]{1,0:T(8,128)(2,1)S(1)} %get-tuple-element.131) | copy-start | bytes 3145732
  580.4 165.3 %all-gather.23.cloned.1.call-start = ((), (), s32[]{:S(2)}) async-start(), calls=%async_computation.7 | async-start | bytes 5242880 | tf_op jit(solution)/shard_map/all_gather | solution.py:83
  597.1 70.9 %collective-permute-start.10 = (bf16[768,4096]{1,0:T(8,128)(2,1)}, bf16[768,4096]{1,0:T(8,128)(2,1)}, u32[]{:S(2)}, u32[]{:S(2)}) collective-permute-start(bf16[768,4096]{1,0:T(8,128)(2,1)} %pad_maximum_fusion.1), channel_id=1, source_target_pairs={{0,8},{8,0},{1,9},{9,1},{2,10},{10,2},{3,11},{11,3},{4,12},{12,4},... | collective-permute-start | bytes 18874376 | tf_op jit(solution)/shard_map/ppermute | solution.py:16
  597.1 70.8 %collective-permute-start.12 = (bf16[2048,768]{1,0:T(8,128)(2,1)}, bf16[2048,768]{1,0:T(8,128)(2,1)}, u32[]{:S(2)}, u32[]{:S(2)}) collective-permute-start(bf16[2048,768]{1,0:T(8,128)(2,1)} %pad_maximum_fusion.8), channel_id=1, source_target_pairs={{0,16},{16,0},{1,17},{17,1},{2,18},{18,2},{3,19},{19,3},{4,20},{20... | collective-permute-start | bytes 9437192 | tf_op jit(solution)/shard_map/ppermute | solution.py:16
  661.1 6.9 copy-start.34
  683.3 10.4 %copy-start.20 = (bf16[2048,256]{1,0:T(8,128)(2,1)S(1)}, bf16[2048,256]{1,0:T(8,128)(2,1)}, u32[]{:S(2)}) copy-start(bf16[2048,256]{1,0:T(8,128)(2,1)} %copy-done.19) | copy-start | bytes 3145732
  683.3 10.4 %copy-start.22 = (bf16[2048,256]{1,0:T(8,128)(2,1)S(1)}, bf16[2048,256]{1,0:T(8,128)(2,1)}, u32[]{:S(2)}) copy-start(bf16[2048,256]{1,0:T(8,128)(2,1)} %copy-done.21) | copy-start | bytes 3145732
  683.3 10.4 %copy-start.24 = (bf16[2048,256]{1,0:T(8,128)(2,1)S(1)}, bf16[2048,256]{1,0:T(8,128)(2,1)}, u32[]{:S(2)}) copy-start(bf16[2048,256]{1,0:T(8,128)(2,1)} %copy-done.23) | copy-start | bytes 3145732
  698.3 71.3 %collective-permute-start.13 = (bf16[2048,768]{1,0:T(8,128)(2,1)}, bf16[2048,768]{1,0:T(8,128)(2,1)}, u32[]{:S(2)}, u32[]{:S(2)}) collective-permute-start(bf16[2048,768]{1,0:T(8,128)(2,1)} %pad_maximum_fusion.9), channel_id=1, source_target_pairs={{0,16},{16,0},{1,17},{17,1},{2,18},{18,2},{3,19},{19,3},{4,20},{20... | collective-permute-start | bytes 9437192 | tf_op jit(solution)/shard_map/ppermute | solution.py:16
  745.7 5.9 copy-start.56
  745.7 5.9 copy-start.57
  748.0 6.3 copy-start.42
  748.0 6.3 slice-start.4
  750.0 85.7 %collective-permute-start.14 = (bf16[2048,768]{1,0:T(8,128)(2,1)}, bf16[2048,768]{1,0:T(8,128)(2,1)}, u32[]{:S(2)}, u32[]{:S(2)}) collective-permute-start(bf16[2048,768]{1,0:T(8,128)(2,1)} %pad_maximum_fusion.10), channel_id=1, source_target_pairs={{0,16},{16,0},{1,17},{17,1},{2,18},{18,2},{3,19},{19,3},{4,20},{20... | collective-permute-start | bytes 9437192 | tf_op jit(solution)/shard_map/ppermute | solution.py:16
  759.3 10.4 %copy-start.43 = (bf16[768,256]{1,0:T(8,128)(2,1)S(1)}, bf16[768,256]{1,0:T(8,128)(2,1)}, u32[]{:S(2)}) copy-start(bf16[768,256]{1,0:T(8,128)(2,1)} %get-tuple-element.64) | copy-start | bytes 1179652
  774.5 61.2 %copy-start.53 = (bf16[768,256]{1,0:T(8,128)(2,1)S(1)}, bf16[768,256]{1,0:T(8,128)(2,1)}, u32[]{:S(2)}) copy-start(bf16[768,256]{1,0:T(8,128)(2,1)} %get-tuple-element.57) | copy-start | bytes 1179652
  774.5 61.2 %copy-start.54 = (bf16[768,256]{1,0:T(8,128)(2,1)S(1)}, bf16[768,256]{1,0:T(8,128)(2,1)}, u32[]{:S(2)}) copy-start(bf16[768,256]{1,0:T(8,128)(2,1)} %get-tuple-element.58) | copy-start | bytes 1179652
  774.5 61.2 %copy-start.68 = (pred[768]{0:T(1024)(128)(4,1)S(1)}, pred[768]{0:T(1024)(128)(4,1)}, u32[]{:S(2)}) copy-start(pred[768]{0:T(1024)(128)(4,1)} %eq.153) | copy-start | bytes 2308
  774.5 61.2 %copy-start.71 = (f32[2048]{0:T(1024)S(1)}, f32[2048]{0:T(1024)}, u32[]{:S(2)}) copy-start(f32[2048]{0:T(1024)} %get-tuple-element.147) | copy-start | bytes 24580
  859.6 9.2 %copy-start.5 = (bf16[768,2048]{1,0:T(8,128)(2,1)S(1)}, bf16[768,2048]{1,0:T(8,128)(2,1)}, u32[]{:S(2)}) copy-start(bf16[768,2048]{1,0:T(8,128)(2,1)} %get-tuple-element.45) | copy-start | bytes 9437188
  859.6 9.2 %copy-start.69 = (pred[768]{0:T(1024)(128)(4,1)S(1)}, pred[768]{0:T(1024)(128)(4,1)}, u32[]{:S(2)}) copy-start(pred[768]{0:T(1024)(128)(4,1)} %eq.153) | copy-start | bytes 2308
  873.6 27.7 %collective-permute-start.15 = (bf16[768,2048]{1,0:T(8,128)(2,1)}, bf16[768,2048]{1,0:T(8,128)(2,1)}, u32[]{:S(2)}, u32[]{:S(2)}) collective-permute-start(bf16[768,2048]{1,0:T(8,128)(2,1)} %get-tuple-element.39), channel_id=1, source_target_pairs={{0,8},{8,0},{1,9},{9,1},{2,10},{10,2},{3,11},{11,3},{4,12},{12,4},... | collective-permute-start | bytes 9437192 | tf_op jit(solution)/shard_map/ppermute | solution.py:16
  (44 other events, 159.4 us)
Sparse Core Ops, SparseCore 0:
  22.1 83.2 all-gather.8
  125.4 78.7 all-gather.10
  209.3 78.7 all-gather.12
  293.1 78.7 all-gather.14
  376.9 78.7 all-gather.16
  478.6 78.8 all-gather.18
  580.5 78.3 all-gather.20
  668.1 77.5 all-gather.22

commit v4 on v3

--- a/solution.py
+++ b/solution.py
@@ -61,7 +61,7 @@
         widths_of[section] = [size * unit for size in sizes]
     mine = lax.dynamic_slice_in_dim(weights[0], core * half, half, 0)
     given = lax.dynamic_slice_in_dim(weights[0], (1 - core) * half, half, 0)
-    lead = widths_of[1][0]
+    lead = sum(widths_of[1][:2])
     lead_given = shifted(columns(given, group * part, lead), "section")
     first_pieces = per_section(columns(mine, group * part, lead), lead_given)
     weight_of = per_section(mine, shifted(after(given, lead_given), "section"))
@@ -77,7 +77,10 @@
         held = []
         start = 0
         for width in widths_of[section]:
-            own = first_pieces[section] if start == 0 else columns(weight_of[section], group * part + start, width)
+            if start + width <= lead:
+                own = first_pieces[section][:, start : start + width]
+            else:
+                own = columns(weight_of[section], group * part + start, width)
             if earlier:
                 own = after(own, tuple(earlier))
             gathered = lax.all_gather(own, "col", axis=1, tiled=True)
@@ -167,8 +170,11 @@
     lower = jnp.where(core == 0, kept, received)
     upper = jnp.where(core == 0, received, kept)
     result = jnp.concatenate([lower, upper], 1).reshape(1, micro, row_count, features)
-    slots = jnp.where(jnp.arange(2)[:, None] == core, steer_part[None], 0.0).reshape(features)
-    steer_total = lax.psum(slots, ("section", "col"))
+    steer_own = lax.psum(steer_part, "col")
+    steer_other = shifted(steer_own, "section")
+    steer_total = jnp.concatenate(
+        [jnp.where(core == 0, steer_own, steer_other), jnp.where(core == 0, steer_other, steer_own)]
+    )
     return (result, steer_total / (MICRO * ROWS))
 
 

time: 921 us -> 893 us (0.970)
  waiting for transfers between devices: 561 us -> 539 us
  blocking collectives: 48.9 us -> 31.4 us
    all_gather x8, waiting for transfers between devices: 404 us -> 376 us  [local(): gathered = lax.all_gather(own, 'col', axis=1, tiled=True)]
    psum x1, blocking collectives: 27 us -> 9.43 us  [local(): steer_own = lax.psum(steer_part, 'col')]
    ppermute x16 -> x17, waiting for transfers between devices: 156 us -> 163 us  [shifted(): lax.ppermute(value, axis, [(source, (source + steps) % count) for source...]
  transfers between devices with their start and end apart: 24 -> 25, of which waited for: 15 -> 17; matrix products, arithmetic and copies ran while one was open for 24% -> 25% of each run, Pallas kernels for 0% -> 0%
where the time goes in v4:
time: 893 us; the launch traced here: 885 us
  waiting for transfers between devices  539 us (60%)
  matrix products  119 us (13%)
  other arithmetic  99.3 us (11%)
  local copies, waits for them, and re-layouts  64.1 us (7%)
  blocking collectives  31.4 us (4%)
  between operations  15.8 us (2%)
  starting transfers between devices  15.7 us (2%)
    all_gather x8, waiting for transfers between devices, local(): gathered = lax.all_gather(own, 'col', axis=1, tiled=True)  376 us
    ppermute x17, waiting for transfers between devices, shifted(): lax.ppermute(value, axis, [(source, (source + steps) % count) for source...  163 us
    dot_general x18, matrix products, times(): lax.dot_general(left, right, (((1,), (1,)), ((), ())), preferred_element_...  119 us
    dynamic_slice x13, local copies, waits for them, and re-layouts, columns(): return lax.dynamic_slice_in_dim(value, start, width, value.ndim - 1)  28.5 us
    psum x2, blocking collectives, local(): sums = lax.psum(tuple(local_sums), ('row', 'section'))  21.9 us
  transfers between devices with their start and end apart: 25, of which 17 were waited for; matrix products, arithmetic and copies ran while one was open for 25% of the time, Pallas kernels for 0%

profile of v4, /device:TPU:0, one launch (start us, length us, event | category | flops | bytes accessed | tf_op | source)
XLA Modules:
  0.0 884.6 jit_solution(1735703050837038713)
XLA Ops:
  7.2 3.1 dynamic-slice_bitcast_fusion.1
  10.8 3.9 collective-permute-done.3
  14.8 4.1 bitcast_select_fusion.2
  20.4 8.4 dynamic-slice_bitcast_fusion
  29.2 74.5 %all-gather.9.cloned.1.call-done = bf16[2048,1024]{1,0:T(8,128)(2,1)} async-done(((bf16[2048,256]{1,0:T(8,128)(2,1)}), bf16[2048,1024]{1,0:T(8,128)(2,1)}) %all-gather.9.cloned.1.call-update) | async-done | bytes 4194320 | tf_op jit(solution)/shard_map/all_gather | solution.py:86
  110.2 11.1 %bitcast_select_fusion = (bf16[2048,2048]{1,0:T(8,128)(2,1)}, bf16[2048,2048]{1,0:T(8,128)(2,1)S(1)}) fusion(bf16[2048,2048]{1,0:T(8,128)(2,1)} %collective-permute-done.4, pred[]{:T(512)S(6)} %eq.141, bf16[1,4096,2048]{2,1,0:T(8,128)(2,1)} %param.8, s32[]{:T(128)S(6)} %select_n.498, pred[]{:T(512)S(6)} %eq.148), kind=kLoop, calls=%fused_computation.65 | loop fusion | flops 8388608 | bytes 33554440 | tf_op jit(solution)/shard_map/jit(_where)/select_n | solution.py:46
  121.3 3.3 copy-done.4
  126.2 61.3 %all-gather.11.cloned.1.call-done = bf16[2048,1024]{1,0:T(8,128)(2,1)} async-done(((bf16[2048,256]{1,0:T(8,128)(2,1)}), bf16[2048,1024]{1,0:T(8,128)(2,1)}) %all-gather.11.cloned.1.call-update) | async-done | bytes 4194320 | tf_op jit(solution)/shard_map/all_gather | solution.py:86
  187.5 2.1 constant_dynamic-slice_fusion.48
  195.5 75.8 %all-gather.13.cloned.1.call-done = bf16[2048,1024]{1,0:T(8,128)(2,1)} async-done(((bf16[2048,256]{1,0:T(8,128)(2,1)}), bf16[2048,1024]{1,0:T(8,128)(2,1)}) %all-gather.13.cloned.1.call-update) | async-done | bytes 4194320 | tf_op jit(solution)/shard_map/all_gather | solution.py:86
  276.4 4.0 constant_dynamic-slice_fusion.54
  285.2 46.4 %collective-permute-done.2 = bf16[768,4096]{1,0:T(8,128)(2,1)} collective-permute-done((bf16[768,4096]{1,0:T(8,128)(2,1)}, bf16[768,4096]{1,0:T(8,128)(2,1)}, u32[]{:S(2)}, u32[]{:S(2)}) %collective-permute-start.2) | collective-permute-done | bytes 6291488 | tf_op jit(solution)/shard_map/ppermute | solution.py:16
  331.5 5.2 broadcast_select_fusion.2
  336.8 2.6 copy-done
  339.4 2.2 copy-done.1
  341.5 2.4 fusion.148
  344.0 11.2 %all-gather.15.cloned.1.call-done = bf16[2048,1024]{1,0:T(8,128)(2,1)} async-done(((bf16[2048,256]{1,0:T(8,128)(2,1)}), bf16[2048,1024]{1,0:T(8,128)(2,1)}) %all-gather.15.cloned.1.call-update) | async-done | bytes 4194320 | tf_op jit(solution)/shard_map/all_gather | solution.py:86
  360.5 3.4 fusion.151
  363.9 4.1 fusion.152
  368.0 2.6 fusion.129
  370.6 4.6 fusion.35
  375.3 11.1 %fusion.31 = f32[768,2048]{1,0:T(8,128)} fusion(bf16[2048,2048]{1,0:T(8,128)(2,1)} %copy-done.4, s32[]{:T(128)S(6)} %select_n.508, bf16[768,4096]{1,0:T(8,128)(2,1)S(1)} %bitcast.28, bf16[768,4096]{1,0:T(8,128)(2,1)S(1)} %bitcast.26), kind=kOutput, calls=%fused_computation.111 | convolution fusion | flops 6448742400 | bytes 27262980 | tf_op jit(solution)/shard_map/dot_general | solution.py:98
  386.4 7.2 add_add_fusion.5
  395.2 2.6 fusion.46
  397.9 4.7 add_add_fusion.4
  402.7 3.9 fusion.57
  406.6 6.5 add_add_fusion.3
  413.1 26.0 %all-gather.17.cloned.1.call-done = bf16[2048,1024]{1,0:T(8,128)(2,1)} async-done(((bf16[2048,256]{1,0:T(8,128)(2,1)}), bf16[2048,1024]{1,0:T(8,128)(2,1)}) %all-gather.17.cloned.1.call-update) | async-done | bytes 4194320 | tf_op jit(solution)/shard_map/all_gather | solution.py:86
  443.9 20.0 %collective-permute-done.8 = bf16[2048,768]{1,0:T(8,128)(2,1)} collective-permute-done((bf16[2048,768]{1,0:T(8,128)(2,1)}, bf16[2048,768]{1,0:T(8,128)(2,1)}, u32[]{:S(2)}, u32[]{:S(2)}) %collective-permute-start.8) | collective-permute-done | bytes 3145760 | tf_op jit(solution)/shard_map/ppermute | solution.py:16
  464.5 7.2 fusion.68
  471.7 12.3 %fusion.23 = (f32[768]{0:T(1024)S(1)}, f32[768]{0:T(1024)S(1)}, f32[768]{0:T(1024)S(1)}, f32[768]{0:T(1024)S(1)}, bf16[768,2048]{1,0:T(8,128)(2,1)}, /*index=5*/f32[768,2048]{1,0:T(8,128)}) fusion(f32[2048]{0:T(1024)S(1)} %dynamic-slice_convert_fusion, bf16[768,4096]{1,0:T(8,128)(2,1)S(1)} %bitcast.35, s32[]{:T(128)S(6)} %select_n.498, ...), kind=kOutput, calls=%fused_computation.87 | convolution fusion | flops 2444620800 | bytes 35812100 | tf_op jit(solution)/shard_map/dot_general | solution.py:98
  484.0 10.9 %all-reduce.1 = (f32[768]{0:T(1024)S(1)}, f32[768]{0:T(1024)S(1)}, f32[768]{0:T(1024)S(1)}, f32[768]{0:T(1024)S(1)}) all-reduce(f32[768]{0:T(1024)S(1)} %get-tuple-element.25, f32[768]{0:T(1024)S(1)} %get-tuple-element.22, f32[768]{0:T(1024)S(1)} %get-tuple-element.23, ...), channel_id=1, replica_groups=mesh['groups'=2,'section'=2,'row'=2,'col'=4] {'row','section'}, use_global_device_ids=true, to_apply=%region_5.6 | all-reduce | flops 3072 | bytes 24576 | tf_op jit(solution)/shard_map/psum | solution.py:131
  497.9 8.7 fusion.29
  508.1 3.0 constant_dynamic-slice_fusion.6
  511.1 31.7 %all-gather.19.cloned.1.call-done = bf16[2048,1024]{1,0:T(8,128)(2,1)} async-done(((bf16[2048,256]{1,0:T(8,128)(2,1)}), bf16[2048,1024]{1,0:T(8,128)(2,1)}) %all-gather.19.cloned.1.call-update) | async-done | bytes 4194320 | tf_op jit(solution)/shard_map/all_gather | solution.py:86
  547.8 18.3 %collective-permute-done.11 = bf16[2048,768]{1,0:T(8,128)(2,1)} collective-permute-done((bf16[2048,768]{1,0:T(8,128)(2,1)}, bf16[2048,768]{1,0:T(8,128)(2,1)}, u32[]{:S(2)}, u32[]{:S(2)}) %collective-permute-start.11) | collective-permute-done | bytes 3145760 | tf_op jit(solution)/shard_map/ppermute | solution.py:16
  566.3 9.4 %collective-permute-done.9 = bf16[768,2048]{1,0:T(8,128)(2,1)} collective-permute-done((bf16[768,2048]{1,0:T(8,128)(2,1)S(1)}, bf16[768,2048]{1,0:T(8,128)(2,1)}, u32[]{:S(2)}, u32[]{:S(2)}) %collective-permute-start.9) | collective-permute-done | bytes 3145760 | tf_op jit(solution)/shard_map/ppermute | solution.py:16
  575.7 2.4 broadcast_select_fusion.5
  578.1 3.8 pad_maximum_fusion.1
  583.8 60.7 %all-gather.21.cloned.1.call-done = bf16[2048,1024]{1,0:T(8,128)(2,1)} async-done(((bf16[2048,256]{1,0:T(8,128)(2,1)}), bf16[2048,1024]{1,0:T(8,128)(2,1)}) %all-gather.21.cloned.1.call-update) | async-done | bytes 4194320 | tf_op jit(solution)/shard_map/all_gather | solution.py:86
  649.4 4.0 collective-permute-done.12
  653.4 6.8 broadcast_select_fusion.1
  660.8 3.3 fusion.186
  664.1 4.6 pad_maximum_fusion
  668.7 9.3 %fusion.33 = f32[768,2048]{1,0:T(8,128)S(1)} fusion(bf16[2048,2048]{1,0:T(8,128)(2,1)} %get-tuple-element.53, bf16[768,8192]{1,0:T(8,128)(2,1)S(1)} %pad_maximum_fusion, s32[]{:T(128)S(6)} %select_n.508), kind=kOutput, calls=%fused_computation.120 | convolution fusion | flops 6442450944 | bytes 17825796 | tf_op jit(solution)/shard_map/dot_general | solution.py:98
  679.1 4.6 fusion.82
  684.1 9.4 %add_add_fusion.2 = f32[768,2048]{1,0:T(8,128)} fusion(f32[768,2048]{1,0:T(8,128)S(1)} %fusion.33, f32[768,2048]{1,0:T(8,128)} %fusion.82, bf16[2048,768]{1,0:T(8,128)(2,1)} %collective-permute-done.11, bf16[768,256]{1,0:T(8,128)(2,1)S(1)} %get-tuple-element.76, bf16[768,256]{1,0:T(8,128)(2,1)} %get-tuple-element.77, ...), kind=kOutput, calls=%fused_computation.101 | convolution fusion | flops 2422603776 | bytes 23199744 | tf_op jit(solution)/shard_map/dot_general | solution.py:98
  693.5 2.9 constant_dynamic-slice_fusion.2
  696.3 34.7 %all-gather.23.cloned.1.call-done = bf16[2048,1024]{1,0:T(8,128)(2,1)} async-done(((bf16[2048,256]{1,0:T(8,128)(2,1)}), bf16[2048,1024]{1,0:T(8,128)(2,1)}) %all-gather.23.cloned.1.call-update) | async-done | bytes 4194320 | tf_op jit(solution)/shard_map/all_gather | solution.py:86
  731.1 2.3 constant_dynamic-slice_fusion.5
  737.0 2.6 fusion.93
  739.7 4.9 add_add_fusion.1
  744.6 4.6 fusion.104
  749.2 5.8 collective-permute-done.13
  755.1 4.8 add_add_fusion
  760.0 7.2 fusion.115
  767.2 54.0 %collective-permute-done.14 = bf16[2048,768]{1,0:T(8,128)(2,1)} collective-permute-done((bf16[2048,768]{1,0:T(8,128)(2,1)}, bf16[2048,768]{1,0:T(8,128)(2,1)}, u32[]{:S(2)}, u32[]{:S(2)}) %collective-permute-start.14) | collective-permute-done | bytes 3145760 | tf_op jit(solution)/shard_map/ppermute | solution.py:16
  821.2 11.6 %fusion.15 = (f32[768]{0:T(1024)}, f32[768]{0:T(1024)}, f32[768]{0:T(1024)}, f32[768]{0:T(1024)}, bf16[768,2048]{1,0:T(8,128)(2,1)}, /*index=5*/f32[768,2048]{1,0:T(8,128)}) fusion(bf16[768,2048]{1,0:T(8,128)(2,1)S(1)} %get-tuple-element.46, f32[2048]{0:T(1024)S(1)} %dynamic-slice_convert_fusion, pred[768]{0:T(1024)(128)(4,1)S(1)} %copy-done.66, ...), kind=kOutput, calls=%fused_computation.79 | convolution fusion | flops 2444620800 | bytes 35812100 | tf_op jit(solution)/shard_map/dot_general | solution.py:98
  832.7 11.0 %all-reduce = (f32[768]{0:T(1024)S(1)}, f32[768]{0:T(1024)S(1)}, f32[768]{0:T(1024)S(1)}, f32[768]{0:T(1024)S(1)}) all-reduce(f32[768]{0:T(1024)} %get-tuple-element.24, f32[768]{0:T(1024)} %get-tuple-element.19, f32[768]{0:T(1024)} %get-tuple-element.20, ...), channel_id=1, replica_groups=mesh['groups'=2,'section'=2,'row'=2,'col'=4] {'row','section'}, use_global_device_ids=true, to_apply=%region_1.2 | all-reduce | flops 3072 | bytes 24576 | tf_op jit(solution)/shard_map/psum | solution.py:131
  845.1 9.2 %select_reduce_fusion = (f32[2048]{0:T(1024)S(1)}, f32[2048]{0:T(1024)S(1)}, f32[768,2048]{1,0:T(8,128)S(1)}) fusion(bf16[768,2048]{1,0:T(8,128)(2,1)} %get-tuple-element.45, f32[768]{0:T(1024)S(1)} %get-tuple-element.41, f32[768]{0:T(1024)S(1)} %get-tuple-element.44, f32[2048]{0:T(1024)S(1)} %dynamic-slice_convert_fusion, pred[768]{0:T(1024)(128)(4,1)} %eq.144, ...), kind=kLoop, calls=%fused_computation.96 | loop fusion | flops 31453184 | bytes 28356096 | tf_op jit(solution)/shard_map/reduce_sum | solution.py:164
  854.4 4.7 broadcast_select_fusion.9
  859.1 9.4 %psum.71 = f32[2048]{0:T(1024)S(1)} all-reduce(f32[2048]{0:T(1024)S(1)} %add.711), channel_id=1, replica_groups=mesh['groups'=2,'section'=2,'row'=2,'col'=4] {'col'}, use_global_device_ids=true, to_apply=%region_18.19 | all-reduce | flops 2048 | bytes 16384 | tf_op jit(solution)/shard_map/psum | solution.py:173
  870.4 3.4 broadcast_select_fusion.8
  873.8 3.5 pad_maximum_fusion.2
  (240 shorter events, 63.2 us)
Async XLA Ops:
  7.2 96.6 %all-gather.9.cloned.1.call-start = ((), (), s32[]{:S(2)}) async-start(), calls=%async_computation | async-start | bytes 5242880 | tf_op jit(solution)/shard_map/all_gather | solution.py:86
  10.3 4.4 collective-permute-start.3
  20.4 167.1 %all-gather.11.cloned.1.call-start = ((), (), s32[]{:S(2)}) async-start(), calls=%async_computation.1 | async-start | bytes 5242880 | tf_op jit(solution)/shard_map/all_gather | solution.py:86
  28.8 81.3 %collective-permute-start.4 = (bf16[2048,2048]{1,0:T(8,128)(2,1)}, bf16[2048,2048]{1,0:T(8,128)(2,1)}, u32[]{:S(2)}, u32[]{:S(2)}) collective-permute-start(bf16[2048,2048]{1,0:T(8,128)(2,1)} %dynamic-slice_bitcast_fusion), channel_id=1, source_target_pairs={{0,8},{8,0},{1,9},{9,1},{2,10},{10,2},{3,11},{11,3},{4,12},{12,4},... | collective-permute-start | bytes 25165832 | tf_op jit(solution)/shard_map/ppermute | solution.py:16
  108.6 162.7 %all-gather.13.cloned.1.call-start = ((), (), s32[]{:S(2)}) async-start(), calls=%async_computation.2 | async-start | bytes 5242880 | tf_op jit(solution)/shard_map/all_gather | solution.py:86
  108.7 83.8 %collective-permute-start.5 = (bf16[2048,768]{1,0:T(8,128)(2,1)}, bf16[2048,768]{1,0:T(8,128)(2,1)}, u32[]{:S(2)}, u32[]{:S(2)}) collective-permute-start(bf16[2048,768]{1,0:T(8,128)(2,1)} %pad_maximum_fusion.3), channel_id=1, source_target_pairs={{0,16},{16,0},{1,17},{17,1},{2,18},{18,2},{3,19},{19,3},{4,20},{20... | collective-permute-start | bytes 9437192 | tf_op jit(solution)/shard_map/ppermute | solution.py:16
  192.4 162.7 %all-gather.15.cloned.1.call-start = ((), (), s32[]{:S(2)}) async-start(), calls=%async_computation.3 | async-start | bytes 5242880 | tf_op jit(solution)/shard_map/all_gather | solution.py:86
  192.5 83.7 %collective-permute-start.6 = (bf16[2048,768]{1,0:T(8,128)(2,1)}, bf16[2048,768]{1,0:T(8,128)(2,1)}, u32[]{:S(2)}, u32[]{:S(2)}) collective-permute-start(bf16[2048,768]{1,0:T(8,128)(2,1)} %pad_maximum_fusion.4), channel_id=1, source_target_pairs={{0,16},{16,0},{1,17},{17,1},{2,18},{18,2},{3,19},{19,3},{4,20},{20... | collective-permute-start | bytes 9437192 | tf_op jit(solution)/shard_map/ppermute | solution.py:16
  194.0 82.3 %copy-start.68 = (bf16[1,4096]{1,0:T(2,128)(2,1)S(1)}, bf16[1,4096]{1,0:T(2,128)(2,1)}, u32[]{:S(2)}) copy-start(bf16[1,4096]{1,0:T(2,128)(2,1)} %param.9) | copy-start | bytes 24580
  194.0 137.5 %collective-permute-start.2 = (bf16[768,4096]{1,0:T(8,128)(2,1)}, bf16[768,4096]{1,0:T(8,128)(2,1)}, u32[]{:S(2)}, u32[]{:S(2)}) collective-permute-start(bf16[768,4096]{1,0:T(8,128)(2,1)} %bitcast.31), channel_id=1, source_target_pairs={{0,4},{4,0},{1,5},{5,1},{2,6},{6,2},{3,7},{7,3},{8,12},{12,8},{9,1... | collective-permute-start | bytes 18874376 | tf_op jit(solution)/shard_map/ppermute | solution.py:16
  274.5 6.4 copy-start.72
  274.5 8.5 copy-start.73
  276.2 162.8 %all-gather.17.cloned.1.call-start = ((), (), s32[]{:S(2)}) async-start(), calls=%async_computation.4 | async-start | bytes 5242880 | tf_op jit(solution)/shard_map/all_gather | solution.py:86
  276.4 6.7 collective-permute-start.1
  280.4 191.2 %collective-permute-start = (bf16[768,2048]{1,0:T(8,128)(2,1)}, bf16[768,2048]{1,0:T(8,128)(2,1)}, u32[]{:S(2)}, u32[]{:S(2)}) collective-permute-start(bf16[768,2048]{1,0:T(8,128)(2,1)} %constant_dynamic-slice_fusion.54), channel_id=1, source_target_pairs={{0,8},{8,0},{1,9},{9,1},{2,10},{10,2},{3,11},{11,3},{4,12},{12,4},... | collective-permute-start | bytes 9437192 | tf_op jit(solution)/shard_map/ppermute | solution.py:16
  281.4 78.7 %collective-permute-start.7 = (bf16[2048,768]{1,0:T(8,128)(2,1)}, bf16[2048,768]{1,0:T(8,128)(2,1)}, u32[]{:S(2)}, u32[]{:S(2)}) collective-permute-start(bf16[2048,768]{1,0:T(8,128)(2,1)} %pad_maximum_fusion.5), channel_id=1, source_target_pairs={{0,16},{16,0},{1,17},{17,1},{2,18},{18,2},{3,19},{19,3},{4,20},{20... | collective-permute-start | bytes 9437192 | tf_op jit(solution)/shard_map/ppermute | solution.py:16
  282.9 188.7 %copy-start.65 = (pred[768]{0:T(1024)(128)(4,1)}, pred[768]{0:T(1024)(128)(4,1)S(1)}, u32[]{:S(2)}) copy-start(pred[768]{0:T(1024)(128)(4,1)S(1)} %eq.147) | copy-start | bytes 2308
  360.2 182.7 %all-gather.19.cloned.1.call-start = ((), (), s32[]{:S(2)}) async-start(), calls=%async_computation.5 | async-start | bytes 5242880 | tf_op jit(solution)/shard_map/all_gather | solution.py:86
  360.4 7.5 slice-start
  360.5 7.5 slice-start.2
  375.3 11.1 %copy-start.52 = (bf16[768,256]{1,0:T(8,128)(2,1)S(1)}, bf16[768,256]{1,0:T(8,128)(2,1)}, u32[]{:S(2)}) copy-start(bf16[768,256]{1,0:T(8,128)(2,1)} %get-tuple-element.90) | copy-start | bytes 1179652
  386.4 8.7 copy-start.11
  386.4 8.7 copy-start.13
  386.4 8.7 copy-start.15
  386.4 8.7 copy-start.62
  386.4 8.7 copy-start.63
  386.4 8.7 copy-start.64
  393.6 70.3 %collective-permute-start.8 = (bf16[2048,768]{1,0:T(8,128)(2,1)}, bf16[2048,768]{1,0:T(8,128)(2,1)}, u32[]{:S(2)}, u32[]{:S(2)}) collective-permute-start(bf16[2048,768]{1,0:T(8,128)(2,1)} %pad_maximum_fusion.6), channel_id=1, source_target_pairs={{0,16},{16,0},{1,17},{17,1},{2,18},{18,2},{3,19},{19,3},{4,20},{20... | collective-permute-start | bytes 9437192 | tf_op jit(solution)/shard_map/ppermute | solution.py:16
  413.1 51.3 %copy-start.39 = (bf16[2048,256]{1,0:T(8,128)(2,1)S(1)}, bf16[2048,256]{1,0:T(8,128)(2,1)}, u32[]{:S(2)}) copy-start(bf16[2048,256]{1,0:T(8,128)(2,1)} %copy-done.38) | copy-start | bytes 3145732
  413.1 51.3 %copy-start.58 = (bf16[768,256]{1,0:T(8,128)(2,1)S(1)}, bf16[768,256]{1,0:T(8,128)(2,1)}, u32[]{:S(2)}) copy-start(bf16[768,256]{1,0:T(8,128)(2,1)} %get-tuple-element.101) | copy-start | bytes 1179652
  441.2 22.7 %copy-start.26 = (bf16[2048,256]{1,0:T(8,128)(2,1)}, bf16[2048,256]{1,0:T(8,128)(2,1)S(1)}, u32[]{:S(2)}) copy-start(bf16[2048,256]{1,0:T(8,128)(2,1)S(1)} %get-tuple-element.132) | copy-start | bytes 3145732
  442.1 29.5 %slice-start.6 = ((s8[6291456]{0:T(1024)(128)(4,1)}), s8[2097152]{0:T(1024)(128)(4,1)S(1)}, s32[]{:S(2)}) async-start(s8[6291456]{0:T(1024)(128)(4,1)} %bitcast.33), calls=%async_computation.14 | async-start | bytes 4194304
  464.0 180.5 %all-gather.21.cloned.1.call-start = ((), (), s32[]{:S(2)}) async-start(), calls=%async_computation.6 | async-start | bytes 5242880 | tf_op jit(solution)/shard_map/all_gather | solution.py:86
  464.4 7.2 slice-start.7
  464.4 7.2 copy-start.59
  464.5 7.2 copy-start.60
  464.5 7.2 copy-start.61
  464.5 7.2 copy-start.70
  496.3 69.8 %collective-permute-start.11 = (bf16[2048,768]{1,0:T(8,128)(2,1)}, bf16[2048,768]{1,0:T(8,128)(2,1)}, u32[]{:S(2)}, u32[]{:S(2)}) collective-permute-start(bf16[2048,768]{1,0:T(8,128)(2,1)} %pad_maximum_fusion.7), channel_id=1, source_target_pairs={{0,16},{16,0},{1,17},{17,1},{2,18},{18,2},{3,19},{19,3},{4,20},{20... | collective-permute-start | bytes 9437192 | tf_op jit(solution)/shard_map/ppermute | solution.py:16
  506.6 69.1 %collective-permute-start.9 = (bf16[768,2048]{1,0:T(8,128)(2,1)S(1)}, bf16[768,2048]{1,0:T(8,128)(2,1)}, u32[]{:S(2)}, u32[]{:S(2)}) collective-permute-start(bf16[768,2048]{1,0:T(8,128)(2,1)S(1)} %get-tuple-element.46), channel_id=1, source_target_pairs={{0,4},{4,0},{1,5},{5,1},{2,6},{6,2},{3,7},{7,3},{8,12},{12,8},{9,1... | collective-permute-start | bytes 9437192 | tf_op jit(solution)/shard_map/ppermute | solution.py:16
  545.0 21.1 %copy-start.32 = (bf16[2048,256]{1,0:T(8,128)(2,1)}, bf16[2048,256]{1,0:T(8,128)(2,1)S(1)}, u32[]{:S(2)}) copy-start(bf16[2048,256]{1,0:T(8,128)(2,1)S(1)} %get-tuple-element.129) | copy-start | bytes 3145732
  566.1 165.0 %all-gather.23.cloned.1.call-start = ((), (), s32[]{:S(2)}) async-start(), calls=%async_computation.7 | async-start | bytes 5242880 | tf_op jit(solution)/shard_map/all_gather | solution.py:86
  582.6 70.9 %collective-permute-start.10 = (bf16[768,4096]{1,0:T(8,128)(2,1)}, bf16[768,4096]{1,0:T(8,128)(2,1)}, u32[]{:S(2)}, u32[]{:S(2)}) collective-permute-start(bf16[768,4096]{1,0:T(8,128)(2,1)} %pad_maximum_fusion.1), channel_id=1, source_target_pairs={{0,8},{8,0},{1,9},{9,1},{2,10},{10,2},{3,11},{11,3},{4,12},{12,4},... | collective-permute-start | bytes 18874376 | tf_op jit(solution)/shard_map/ppermute | solution.py:16
  582.6 70.8 %collective-permute-start.12 = (bf16[2048,768]{1,0:T(8,128)(2,1)}, bf16[2048,768]{1,0:T(8,128)(2,1)}, u32[]{:S(2)}, u32[]{:S(2)}) collective-permute-start(bf16[2048,768]{1,0:T(8,128)(2,1)} %pad_maximum_fusion.8), channel_id=1, source_target_pairs={{0,16},{16,0},{1,17},{17,1},{2,18},{18,2},{3,19},{19,3},{4,20},{20... | collective-permute-start | bytes 9437192 | tf_op jit(solution)/shard_map/ppermute | solution.py:16
  646.6 6.8 copy-start.37
  668.7 10.4 %copy-start.23 = (bf16[2048,256]{1,0:T(8,128)(2,1)S(1)}, bf16[2048,256]{1,0:T(8,128)(2,1)}, u32[]{:S(2)}) copy-start(bf16[2048,256]{1,0:T(8,128)(2,1)} %copy-done.22) | copy-start | bytes 3145732
  668.7 10.4 %copy-start.25 = (bf16[2048,256]{1,0:T(8,128)(2,1)S(1)}, bf16[2048,256]{1,0:T(8,128)(2,1)}, u32[]{:S(2)}) copy-start(bf16[2048,256]{1,0:T(8,128)(2,1)} %copy-done.24) | copy-start | bytes 3145732
  668.7 10.4 %copy-start.27 = (bf16[2048,256]{1,0:T(8,128)(2,1)S(1)}, bf16[2048,256]{1,0:T(8,128)(2,1)}, u32[]{:S(2)}) copy-start(bf16[2048,256]{1,0:T(8,128)(2,1)} %copy-done.26) | copy-start | bytes 3145732
  683.7 71.3 %collective-permute-start.13 = (bf16[2048,768]{1,0:T(8,128)(2,1)}, bf16[2048,768]{1,0:T(8,128)(2,1)}, u32[]{:S(2)}, u32[]{:S(2)}) collective-permute-start(bf16[2048,768]{1,0:T(8,128)(2,1)} %pad_maximum_fusion.9), channel_id=1, source_target_pairs={{0,16},{16,0},{1,17},{17,1},{2,18},{18,2},{3,19},{19,3},{4,20},{20... | collective-permute-start | bytes 9437192 | tf_op jit(solution)/shard_map/ppermute | solution.py:16
  731.1 5.9 copy-start.55
  731.1 5.9 copy-start.56
  731.1 5.9 copy-start.57
  733.4 6.3 copy-start.45
  733.4 6.3 slice-start.4
  735.4 85.8 %collective-permute-start.14 = (bf16[2048,768]{1,0:T(8,128)(2,1)}, bf16[2048,768]{1,0:T(8,128)(2,1)}, u32[]{:S(2)}, u32[]{:S(2)}) collective-permute-start(bf16[2048,768]{1,0:T(8,128)(2,1)} %pad_maximum_fusion.10), channel_id=1, source_target_pairs={{0,16},{16,0},{1,17},{17,1},{2,18},{18,2},{3,19},{19,3},{4,20},{20... | collective-permute-start | bytes 9437192 | tf_op jit(solution)/shard_map/ppermute | solution.py:16
  744.6 10.4 %copy-start.46 = (bf16[768,256]{1,0:T(8,128)(2,1)S(1)}, bf16[768,256]{1,0:T(8,128)(2,1)}, u32[]{:S(2)}) copy-start(bf16[768,256]{1,0:T(8,128)(2,1)} %get-tuple-element.64) | copy-start | bytes 1179652
  759.9 61.2 %copy-start.53 = (bf16[768,256]{1,0:T(8,128)(2,1)S(1)}, bf16[768,256]{1,0:T(8,128)(2,1)}, u32[]{:S(2)}) copy-start(bf16[768,256]{1,0:T(8,128)(2,1)} %get-tuple-element.57) | copy-start | bytes 1179652
  759.9 61.2 %copy-start.54 = (bf16[768,256]{1,0:T(8,128)(2,1)S(1)}, bf16[768,256]{1,0:T(8,128)(2,1)}, u32[]{:S(2)}) copy-start(bf16[768,256]{1,0:T(8,128)(2,1)} %get-tuple-element.58) | copy-start | bytes 1179652
  760.0 61.2 %copy-start.66 = (pred[768]{0:T(1024)(128)(4,1)S(1)}, pred[768]{0:T(1024)(128)(4,1)}, u32[]{:S(2)}) copy-start(pred[768]{0:T(1024)(128)(4,1)} %eq.144) | copy-start | bytes 2308
  760.0 61.2 %copy-start.69 = (f32[2048]{0:T(1024)S(1)}, f32[2048]{0:T(1024)}, u32[]{:S(2)}) copy-start(f32[2048]{0:T(1024)} %get-tuple-element.151) | copy-start | bytes 24580
  845.1 9.2 %copy-start.5 = (bf16[768,2048]{1,0:T(8,128)(2,1)S(1)}, bf16[768,2048]{1,0:T(8,128)(2,1)}, u32[]{:S(2)}) copy-start(bf16[768,2048]{1,0:T(8,128)(2,1)} %get-tuple-element.45) | copy-start | bytes 9437188
  845.1 9.2 %copy-start.67 = (pred[768]{0:T(1024)(128)(4,1)S(1)}, pred[768]{0:T(1024)(128)(4,1)}, u32[]{:S(2)}) copy-start(pred[768]{0:T(1024)(128)(4,1)} %eq.144) | copy-start | bytes 2308
  859.1 11.3 %collective-permute-start.15 = (bf16[768,2048]{1,0:T(8,128)(2,1)}, bf16[768,2048]{1,0:T(8,128)(2,1)}, u32[]{:S(2)}, u32[]{:S(2)}) collective-permute-start(bf16[768,2048]{1,0:T(8,128)(2,1)} %get-tuple-element.39), channel_id=1, source_target_pairs={{0,8},{8,0},{1,9},{9,1},{2,10},{10,2},{3,11},{11,3},{4,12},{12,4},... | collective-permute-start | bytes 9437192 | tf_op jit(solution)/shard_map/ppermute | solution.py:16
  868.6 1.2 collective-permute-start.16
  (43 other events, 138.6 us)
Sparse Core Ops, SparseCore 0:
  20.5 83.1 all-gather.8
  108.7 78.7 all-gather.10
  192.6 78.7 all-gather.12
  276.4 78.7 all-gather.14
  360.3 78.7 all-gather.16
  464.1 78.7 all-gather.18
  566.2 78.2 all-gather.20
  653.6 77.4 all-gather.22
